TPU v7x, 128 devices: a whole 4x4x4 slice. The times are simulated.
128 devices in a mesh: rows: 16 (over x, z), mlp: 8 (over y, core).
Axes of the slice: x: 4, y: 4, z: 4, core: 2. Of those that a mesh axis runs over, the one named last changes fastest.
Arguments:
- tokens: bfloat16 [32768, 1408], P(('rows', 'mlp')), may hold values from -6 to 6
- norm_gain: float32 [3, 1408], replicated, may hold values from 0.1 to 1.9
- norm_bias: float32 [3, 1408], replicated, may hold values from -2 to 2
- input_weight: bfloat16 [1408, 4224], replicated, may hold values from -0.15625 to 0.15625
- input_bias: float32 [4224], replicated, may hold values from -36 to 36
- output_weight: bfloat16 [1408, 1408], replicated, may hold values from -0.15625 to 0.15625
- expand_weight: bfloat16 [6144, 1408], P('rows'), may hold values from -0.15625 to 0.15625
- reduce_weight: bfloat16 [6144, 1408], P('rows'), may hold values from -0.078125 to 0.078125
- merger_weight: bfloat16 [5632, 4096], P(None, 'mlp'), may hold values from -1 to 1
- output_gain: float32 [4096], P('mlp'), may hold values from 0.1 to 1.9
- segments: int32 [32768], P(('rows', 'mlp')), may hold values from 0 to 4, as said below
- grid_sides: int32 [512, 2], P('rows'), may hold values from 0 to 8, as said below
- routes: int32 [8192, 1], P('rows'), may hold values from 0 to 127; in each aligned block of 512 rows (0 to 511, 512 to 1023, ...) at most 8 rows name the same one
Outputs:
- delivered: bfloat16 [16384, 4096], P(('rows', 'mlp'))
- peaks: float32 [512], P(('rows', 'mlp'))
Inputs may be any that keep to these rules, and one draw needn't show every extreme that they name: `grid_sides`: every device has 4 request slots; a present request has even height and width of 2 to 8, an absent slot 0 and 0; each device holds 1 to 4 requests, whose 1 + height * width tokens together fit in its 256 token slots; some request is 8 x 8. A device's tokens hold its present requests in slot order from its first token on, each as a class token followed by its height x width patches in row-major order; segments gives the slot number of each such token and 4 for the remaining padding tokens. `routes`: in each aligned block of 512 merged rows (the merged rows of 8 consecutive devices) no destination is named more than 8 times; in some block some destination is named exactly 8 times. Zero merged rows have destinations too.
All inputs are finite; a program needn't handle non-finite values.
Results may differ from a plain program's by a relative error of at most 0.012.
The roundings to bfloat16 on the way count: a program that leaves them out, or rounds other values in their place, can miss the bound.
Values may be sent and summed in bfloat16 or wider, within the bound.
A program may use at most 192 MiB of HBM per device.

v0:
```python
import math

import jax
import jax.numpy as jnp
from jax import lax
from jax.sharding import PartitionSpec as P

HEADS = 16
HEAD = 88
OUT = 4096
REQ_DEV = 4
MERGED_DEV = 64


EPS = 1e-06


def combined_all(part, axis, combine):
    gathered = jax.tree.map(lambda a: lax.all_gather(a, axis), part)

    def take(source):
        return jax.tree.map(lambda a: lax.dynamic_index_in_dim(a, source, 0, False), gathered)

    return lax.fori_loop(
        1, lax.axis_size(axis), lambda source, state: combine(state, take(source)), take(0)
    )


def layer_norm(values, gain, bias):
    mean_value = jnp.mean(values, axis=-1, keepdims=True)
    centered = values - mean_value
    variance = jnp.mean(centered * centered, axis=-1, keepdims=True)
    return centered * lax.rsqrt(variance + EPS) * gain + bias


def merge_layout(grid_block):
    heights = grid_block[:, 0]
    widths_all = grid_block[:, 1]
    lengths = jnp.where(heights > 0, 1 + heights * widths_all, 0)
    starts = jnp.cumsum(lengths) - lengths
    counts = heights // 2 * (widths_all // 2)
    merge_starts = jnp.cumsum(counts) - counts
    merge_ends = merge_starts + counts
    merge_slots = jnp.arange(MERGED_DEV, dtype=jnp.int32)
    owner_slot = jnp.sum((merge_ends[None, :] <= merge_slots[:, None]).astype(jnp.int32), axis=1)
    is_valid = owner_slot < REQ_DEV
    chosen = (owner_slot[:, None] == jnp.arange(REQ_DEV, dtype=jnp.int32)[None, :]).astype(
        jnp.int32
    )
    row_width = jnp.sum(chosen * widths_all[None, :], axis=1)
    row_start = jnp.sum(chosen * starts[None, :], axis=1)
    row_merge = jnp.sum(chosen * merge_starts[None, :], axis=1)
    within = merge_slots - row_merge
    half_width = jnp.maximum(row_width // 2, 1)
    patch_row = within // half_width
    patch_col = within - patch_row * half_width
    corner = row_start + 1 + 2 * patch_row * row_width + 2 * patch_col
    token_index = jnp.stack(
        [corner, corner + 1, corner + row_width, corner + row_width + 1], axis=1
    )
    token_index = jnp.where(is_valid[:, None], token_index, 0)
    return (token_index, is_valid, owner_slot, counts)


def combine_totals(earlier, latter):
    return (earlier[0] + latter[0], jnp.maximum(earlier[1], latter[1]))


def per_device(
    tokens,
    norm_gain,
    norm_bias,
    input_weight,
    input_bias,
    output_weight,
    expand_weight,
    reduce_weight,
    merger_weight,
    output_gain,
    segments,
    grid_sides,
    routes,
):
    rows_here = tokens.shape[0]
    features = tokens.shape[1]
    n_rows = lax.axis_size("rows")
    n_mlp = lax.axis_size("mlp")
    member = lax.axis_index("mlp")
    residual_in = tokens.astype(jnp.float32)
    normed_in = layer_norm(residual_in, norm_gain[0], norm_bias[0]).astype(jnp.bfloat16)
    joint = (
        jnp.dot(normed_in, input_weight, preferred_element_type=jnp.float32) + input_bias
    ).astype(jnp.bfloat16)
    queries = joint[:, :features].reshape(rows_here, HEADS, HEAD)
    keys_all = joint[:, features : 2 * features].reshape(rows_here, HEADS, HEAD)
    values_all = joint[:, 2 * features :].reshape(rows_here, HEADS, HEAD)
    scores = jnp.einsum(
        "thd,uhd->htu", queries, keys_all, preferred_element_type=jnp.float32
    ) / math.sqrt(HEAD)
    allowed = segments[:, None] == segments[None, :]
    scores = jnp.where(allowed[None], scores, -jnp.inf)
    row_max = jnp.max(scores, axis=-1, keepdims=True)
    weights = jnp.exp(scores - row_max)
    softmax_out = (weights / jnp.sum(weights, axis=-1, keepdims=True)).astype(jnp.bfloat16)
    attended = jnp.einsum(
        "htu,uhd->thd", softmax_out, values_all, preferred_element_type=jnp.float32
    )
    attended = attended.astype(jnp.bfloat16).reshape(rows_here, features)
    residual_mid = residual_in + jnp.dot(
        attended, output_weight, preferred_element_type=jnp.float32
    )
    normed_mid = layer_norm(residual_mid, norm_gain[1], norm_bias[1]).astype(jnp.bfloat16)
    contract = (((1,), (1,)), ((), ()))
    pre_act = lax.dot_general(
        normed_mid,
        lax.all_gather(expand_weight, "rows", axis=0, tiled=True),
        contract,
        preferred_element_type=jnp.float32,
    )
    hidden = jax.nn.gelu(pre_act, approximate=False).astype(jnp.bfloat16)
    unit_out = jnp.dot(
        hidden,
        lax.all_gather(reduce_weight, "rows", axis=0, tiled=True),
        preferred_element_type=jnp.float32,
    )
    residual_out = residual_mid + unit_out
    normed_out = layer_norm(residual_out, norm_gain[2], norm_bias[2]).astype(jnp.bfloat16)
    own_grid = lax.dynamic_slice_in_dim(grid_sides, member * REQ_DEV, REQ_DEV, 0)
    token_index, is_valid, owner_slot, own_counts = merge_layout(own_grid)
    picked = jnp.take(normed_out, token_index.reshape(-1), axis=0).reshape(
        token_index.shape[0], 4 * features
    )
    merged = jnp.where(is_valid[:, None], picked, jnp.zeros_like(picked))
    projected = jnp.dot(
        lax.all_gather(merged, "mlp", axis=0, tiled=True),
        merger_weight,
        preferred_element_type=jnp.float32,
    )
    group_index, group_valid, group_owner, group_counts = jax.vmap(merge_layout)(
        grid_sides.reshape(n_mlp, REQ_DEV, 2)
    )
    group_requests = n_mlp * REQ_DEV
    member_base = (REQ_DEV * jnp.arange(n_mlp, dtype=jnp.int32))[:, None]
    request_of_row = jnp.where(group_valid, group_owner + member_base, group_requests).reshape(-1)
    counts = group_counts.reshape(-1)
    gained = projected * output_gain
    row_squares = jnp.sum(projected * projected, axis=1)
    row_peaks = jnp.max(gained, axis=1)
    member_of = jnp.arange(group_requests, dtype=jnp.int32)[:, None] == request_of_row[None, :]
    sums_part = jnp.sum(jnp.where(member_of, row_squares[None, :], 0.0), axis=1)
    peaks_part = jnp.max(jnp.where(member_of, row_peaks[None, :], -jnp.inf), axis=1)
    square_sum, peak_all = combined_all((sums_part, peaks_part), "mlp", combine_totals)
    inv_rms = lax.rsqrt(square_sum / (jnp.maximum(counts, 1).astype(jnp.float32) * OUT) + EPS)
    row_inv = jnp.sum(jnp.where(member_of, inv_rms[:, None], 0.0), axis=0)
    scaled = (gained * row_inv[:, None]).astype(jnp.bfloat16)
    peak_values = jnp.where(counts > 0, peak_all * inv_rms, 0.0)
    peaks_own = lax.dynamic_slice_in_dim(peak_values, member * REQ_DEV, REQ_DEV, 0)
    targets = routes[:, 0]
    group_rows = targets.shape[0]
    row_order = jnp.arange(group_rows, dtype=jnp.int32)
    same_target = (targets[:, None] == targets[None, :]) & (row_order[None, :] < row_order[:, None])
    target_rank = jnp.sum(same_target.astype(jnp.int32), axis=1)
    devices = n_rows * n_mlp
    capacity = max(2, 2 * MERGED_DEV // n_rows)
    slot_key = target_rank * devices + targets
    selector = (
        jnp.arange(capacity * devices, dtype=jnp.int32)[:, None] == slot_key[None, :]
    ).astype(jnp.bfloat16)
    outgoing = jnp.dot(selector, scaled, preferred_element_type=jnp.float32).astype(jnp.bfloat16)
    outgoing = outgoing.reshape(capacity, devices, scaled.shape[1])
    arrived = lax.all_to_all(outgoing, ("rows", "mlp"), split_axis=1, concat_axis=2, tiled=True)
    delivered = arrived.reshape(capacity * n_rows, n_mlp * scaled.shape[1])
    return (delivered, peaks_own)


def solution(mesh):
    return jax.shard_map(
        per_device,
        mesh=mesh,
        in_specs=(
            P(("rows", "mlp"), None),
            P(),
            P(),
            P(),
            P(),
            P(),
            P("rows", None),
            P("rows", None),
            P(None, "mlp"),
            P("mlp"),
            P(("rows", "mlp")),
            P("rows", None),
            P("rows", None),
        ),
        out_specs=(P(("rows", "mlp"), None), P(("rows", "mlp"))),
        check_vma=False,
    )
```

profile of v0, /device:TPU:1, one launch (start us, length us, event | category | flops | bytes accessed | tf_op | source)
XLA Modules:
  0.0 370.4 jit_solution(16699197834733272568)
XLA Ops:
  7.2 0.7 all-gather.6.cloned.1.call-update
  7.9 0.7 all-gather.8.cloned.1.call-update
  8.7 1.0 slice_reduce_fusion
  9.7 1.3 convert_reduce_fusion
  10.9 1.4 fusion.56
  12.4 8.3 %fusion.1 = bf16[256,4224]{1,0:T(8,128)(2,1)S(1)} fusion(bf16[1408,4224]{1,0:T(8,128)(2,1)} %param.18, f32[4224]{0:T(1024)} %param.19, bf16[256,1408]{1,0:T(8,128)(2,1)} %param.15, f32[1408]{0:T(1024)S(1)} %get-tuple-element.143, f32[1408]{0:T(1024)S(1)} %get-tuple-element.190, f32[256]{0:T(256)S(1)} %add_rsqrt_fusion.2, f32[256]{0:T(256)S(1)} %broadcast_multiply_fusion.2), kind=kOutput, calls=%fused_computation.6 | convolution fusion | flops 3049390080 | bytes 14808576 | tf_op jit(solution)/shard_map/dot_general | solution.py:92
  20.9 0.3 copy.55
  23.5 3.6 fusion.125
  27.0 2.8 fusion.60
  29.9 0.8 copy-done.4
  30.7 1.5 fusion.126
  32.2 0.3 multiply_reduce_fusion.1
  32.5 94.7 %all-gather.6.cloned.1.call-done = bf16[6144,1408]{1,0:T(8,128)(2,1)} async-done(((bf16[384,1408]{1,0:T(8,128)(2,1)}), bf16[6144,1408]{1,0:T(8,128)(2,1)}) %all-gather.6.cloned.1.call-update) | async-done | bytes 17301520 | tf_op jit(solution)/shard_map/all_gather | solution.py:116
  127.2 115.8 %all-gather.8.cloned.1.call-done = bf16[6144,1408]{1,0:T(8,128)(2,1)} async-done(((bf16[384,1408]{1,0:T(8,128)(2,1)}), bf16[6144,1408]{1,0:T(8,128)(2,1)}) %all-gather.8.cloned.1.call-update) | async-done | bytes 17301520 | tf_op jit(solution)/shard_map/all_gather | solution.py:123
  243.1 26.1 %fusion.127 = (f32[256]{0:T(256)S(1)}, f32[256,1408]{1,0:T(8,128)S(1)}) fusion(f32[256,1408]{1,0:T(8,128)S(1)} %get-tuple-element.185, bf16[6144,1408]{1,0:T(8,128)(2,1)} %all-gather.8.cloned.1.call-done, bf16[6144,1408]{1,0:T(8,128)(2,1)} %all-gather.6.cloned.1.call-done, f32[1408]{0:T(1024)S(1)} %get-tuple-element.144, f32[1408]{0:T(1024)S(1)} %get-tuple-element.189, ...), kind=kOutput, calls=%fused_computation.242 | convolution fusion | flops 8963129344 | bytes 37500928 | tf_op jit(solution)/shard_map/dot_general | solution.py:121
  269.1 0.3 multiply_reduce_fusion
  269.5 0.3 add_convert_fusion
  269.8 1.3 gather_fusion
  271.1 0.5 gather.7
  271.6 1.0 select_select_fusion
  273.3 0.7 dynamic-slice
  275.0 36.6 %all-gather.10.cloned.1.call-done = bf16[512,5632]{1,0:T(8,128)(2,1)} async-done(((bf16[64,5632]{1,0:T(8,128)(2,1)}), bf16[512,5632]{1,0:T(8,128)(2,1)}) %all-gather.10.cloned.1.call-update) | async-done | bytes 5767184 | tf_op jit(solution)/shard_map/all_gather | solution.py:135
  311.6 8.1 %multiply_reduce_fusion.3 = (f32[512]{0:T(512)S(1)}, f32[512]{0:T(512)S(1)}, f32[512,512]{0,1:T(8,128)S(1)}) fusion(f32[512]{0:T(512)S(1)} %copy-done.5, bf16[512,5632]{1,0:T(8,128)(2,1)} %all-gather.10.cloned.1.call-done, bf16[5632,512]{1,0:T(8,128)(2,1)} %param.23), kind=kOutput, calls=%fused_computation.88 | convolution fusion | flops 2953837568 | bytes 12589056 | tf_op jit(solution)/shard_map/dot_general | solution.py:134
  320.1 0.4 dynamic-update-slice
  320.5 12.0 %all-reduce.2 = (f32[256]{0:T(256)S(1)}, f32[256]{0:T(256)S(1)}) all-reduce(f32[256]{0:T(256)S(1)} %dynamic-update-slice, f32[256]{0:T(256)S(1)} %dynamic-update-slice.1), channel_id=2, replica_groups=mesh['rows'=16,'mlp'=8] {'mlp'}, use_global_device_ids=true, to_apply=%add | all-reduce | flops 512 | bytes 4096
  333.1 0.8 fusion.55
  333.9 1.5 copy.61
  335.5 7.7 %all-to-all-start = ((bf16[8,128,512]{2,0,1:T(8,128)(2,1)}), bf16[8,128,512]{2,0,1:T(8,128)(2,1)S(1)}, u32[]{:S(2)}, u32[]{:S(2)}) async-start(bf16[8,128,512]{2,0,1:T(8,128)(2,1)} %copy.61), calls=%async_computation | async-start | bytes 2097152 | tf_op jit(solution)/shard_map/all_to_all | solution.py:171
  343.2 0.6 dynamic_slice.36
  343.8 18.4 %all-to-all-done = bf16[8,128,512]{2,0,1:T(8,128)(2,1)S(1)} async-done(((bf16[8,128,512]{2,0,1:T(8,128)(2,1)}), bf16[8,128,512]{2,0,1:T(8,128)(2,1)S(1)}, u32[]{:S(2)}, u32[]{:S(2)}) %all-to-all-start) | async-done | bytes 1048608 | tf_op jit(solution)/shard_map/all_to_all | solution.py:171
  362.2 0.3 copy.62
  362.5 1.3 reshape.533
  (77 shorter events, 4.5 us)
Async XLA Ops:
  7.2 120.1 %all-gather.6.cloned.1.call-start = ((), (), s32[]{:S(2)}) async-start(), calls=%async_computation.1 | async-start | bytes 18382848 | tf_op jit(solution)/shard_map/all_gather | solution.py:116
  7.9 235.2 %all-gather.8.cloned.1.call-start = ((), (), s32[]{:S(2)}) async-start(), calls=%async_computation.2 | async-start | bytes 18382848 | tf_op jit(solution)/shard_map/all_gather | solution.py:123
  8.6 302.9 %all-gather.10.cloned.1.call-start = ((), (), s32[]{:S(2)}) async-start(), calls=%async_computation.3 | async-start | bytes 6488064 | tf_op jit(solution)/shard_map/all_gather | solution.py:135
  20.7 1.1 copy-start.3
  20.7 2.7 copy-start.2
  27.0 2.8 copy-start
  27.0 3.6 copy-start.4
  269.4 3.9 %copy-start.6 = (u32[128]{0:T(128)S(1)}, u32[128]{0:T(128)}, u32[]{:S(2)}) copy-start(u32[128]{0:T(128)} %constant.225) | copy-start | bytes 1540
  269.5 5.2 %copy-start.1 = (s32[512,1]{0,1:T(1,128)S(1)}, s32[512,1]{0,1:T(1,128)}, u32[]{:S(2)}) copy-start(s32[512,1]{0,1:T(1,128)} %param.27) | copy-start | bytes 6148
  269.5 42.1 %copy-start.5 = (f32[512]{0:T(512)S(1)}, f32[512]{0:T(512)}, u32[]{:S(2)}) copy-start(f32[512]{0:T(512)} %param.24) | copy-start | bytes 6148
  335.5 26.8 %all-to-all-start = ((bf16[8,128,512]{2,0,1:T(8,128)(2,1)}), bf16[8,128,512]{2,0,1:T(8,128)(2,1)S(1)}, u32[]{:S(2)}, u32[]{:S(2)}) async-start(bf16[8,128,512]{2,0,1:T(8,128)(2,1)} %copy.61), calls=%async_computation | async-start | bytes 2097152 | tf_op jit(solution)/shard_map/all_to_all | solution.py:171
Sparse Core Ops, SparseCore 0:
  10.2 117.0 all-gather.5
  129.4 113.5 all-gather.7
  272.8 38.7 all-gather.9
where the time goes:
time: 371 us; the launch traced here: 370 us
  waiting for transfers between devices  267 us (72%)
  matrix products  51.2 us (14%)
  between operations  14.7 us (4%)
  blocking collectives  12 us (3%)
  local copies, waits for them, and re-layouts  11.1 us (3%)
  starting transfers between devices  7.86 us (2%)
  other arithmetic  6.35 us (2%)
    all_gather x1, waiting for transfers between devices, per_device(): lax.all_gather(reduce_weight, 'rows', axis=0, tiled=True)  116 us
    all_gather x1, waiting for transfers between devices, per_device(): lax.all_gather(expand_weight, 'rows', axis=0, tiled=True)  94.7 us
    all_gather x1, waiting for transfers between devices, per_device(): lax.all_gather(merged, 'mlp', axis=0, tiled=True)  36.6 us
    dot_general x1, matrix products, per_device(): jnp.dot(hidden, lax.all_gather(reduce_weight, 'rows', axis=0, tiled=True)...  26.1 us
    all_to_all x1, waiting for transfers between devices, per_device(): lax.all_to_all(outgoing, ('rows', 'mlp'), split_axis=1, concat_axis=2, ti...  18.4 us
    unnamed x1, blocking collectives  12 us
    dot_general x1, matrix products, per_device(): jnp.dot(normed_in, input_weight, preferred_element_type=jnp.float32)  8.29 us
    dot_general x1, matrix products, per_device(): jnp.dot(lax.all_gather(merged, 'mlp', axis=0, tiled=True), merger_weight,...  8.11 us
  transfers between devices with their start and end apart: 4, of which 4 were waited for; matrix products, arithmetic and copies ran while one was open for 7% of the time, Pallas kernels for 0%

commit v1 on v0

--- a/solution.py
+++ b/solution.py
@@ -3,6 +3,8 @@
 import jax
 import jax.numpy as jnp
 from jax import lax
+from jax.experimental import pallas as pl
+from jax.experimental.pallas import tpu as pltpu
 from jax.sharding import PartitionSpec as P
 
 HEADS = 16
@@ -24,13 +26,6 @@
     return lax.fori_loop(
         1, lax.axis_size(axis), lambda source, state: combine(state, take(source)), take(0)
     )
-
-
-def layer_norm(values, gain, bias):
-    mean_value = jnp.mean(values, axis=-1, keepdims=True)
-    centered = values - mean_value
-    variance = jnp.mean(centered * centered, axis=-1, keepdims=True)
-    return centered * lax.rsqrt(variance + EPS) * gain + bias
 
 
 def merge_layout(grid_block):
@@ -64,6 +59,361 @@
 
 def combine_totals(earlier, latter):
     return (earlier[0] + latter[0], jnp.maximum(earlier[1], latter[1]))
+
+
+MESH = pl.DeviceIdType.MESH
+PLANE = 144
+HALF = 80
+SHARE = 16
+SLOT = 192
+
+
+def layer_kernel(
+    tokens, gain, bias, wq_hbm, bq, wo_hbm, wa_hbm, wb_hbm, seg, idx, merged_out,
+    wa, wb, wq, wo, joint, acts, resid, acc, att, maskb, psend, precv,
+    send, recv, local,
+):
+    row = lax.axis_index("rows")
+    member = lax.axis_index("mlp")
+    x, z = row // 4, row % 4
+    y, core = member // 2, member % 2
+    features = tokens.shape[1]
+    rows_here = tokens.shape[0]
+
+    def plane(dx, dz):
+        return (((x + dx + 4) % 4) * 4 + (z + dz + 4) % 4, member)
+
+    def column(dy):
+        return (row, ((y + dy + 4) % 4) * 2 + core)
+
+    partner = (row, member + 1 - 2 * core)
+    near = [plane(1, 0), plane(-1, 0), plane(0, 1), plane(0, -1), column(1), column(-1), partner]
+
+    started = []
+
+    def load(src, dst):
+        copy = pltpu.make_async_copy(src, dst, local.at[len(started)])
+        copy.start()
+        started.append(copy)
+        return copy
+
+    own = []
+    first = SLOT - 4 * SHARE
+    for hbm, vmem in ((wa_hbm, wa), (wb_hbm, wb)):
+        base = pl.multiple_of(core * SLOT, 16)
+        own.append(load(hbm.at[pl.ds(base, first)], vmem.at[0, 0, pl.ds(0, first)]))
+        for place, offset in enumerate((0, -1, 1, 2)):
+            at = pl.multiple_of(core * SLOT + first + SHARE * ((y + offset + 4) % 4), 16)
+            own.append(
+                load(hbm.at[pl.ds(at, SHARE)], vmem.at[0, 0, pl.ds(first + place * SHARE, SHARE)])
+            )
+    chunk = 384
+    parts = wq_hbm.shape[1] // chunk
+    first_wq = len(started)
+    for j in range(parts):
+        load(wq_hbm.at[:, pl.ds(j * chunk, chunk)], wq.at[:, pl.ds(j * chunk, chunk)])
+    wo_copy = load(wo_hbm, wo)
+
+    barrier = pltpu.get_barrier_semaphore()
+    for device in near:
+        pl.semaphore_signal(barrier, inc=1, device_id=device, device_id_type=MESH)
+    pl.semaphore_wait(barrier, len(near))
+
+    sent = []
+
+    def push(src, dst, device):
+        k = len(sent)
+        copy = pltpu.make_async_remote_copy(
+            src_ref=src, dst_ref=dst, send_sem=send.at[k], recv_sem=recv.at[k],
+            device_id=device, device_id_type=MESH,
+        )
+        copy.start()
+        sent.append(copy)
+        return copy
+
+    def slot_a(i, k):
+        return wa.at[k, i]
+
+    def slot_b(i, k):
+        return wb.at[i, k]
+
+    def step_x(s):
+        return plane(s, 0)
+
+    def step_z(s):
+        return plane(0, s)
+
+    weights = ((slot_a, step_x, step_z), (slot_b, step_z, step_x))
+    up, low, whole = pl.ds(0, HALF), pl.ds(HALF, PLANE - HALF), pl.ds(0, PLANE)
+
+    def send_first(w):
+        slot, one, _ = w
+        return [
+            push(slot(0, 0).at[whole], slot(3, 0).at[whole], one(1)),
+            push(slot(0, 0).at[whole], slot(1, 0).at[whole], one(-1)),
+        ]
+
+    def forward_first(w):
+        slot, one, _ = w
+        return [
+            push(slot(3, 0).at[up], slot(2, 0).at[up], one(1)),
+            push(slot(1, 0).at[low], slot(2, 0).at[low], one(-1)),
+        ]
+
+    def send_second(w, i):
+        slot, _, two = w
+        return [
+            push(slot(i, 0).at[whole], slot(i, 3).at[whole], two(1)),
+            push(slot(i, 0).at[whole], slot(i, 1).at[whole], two(-1)),
+        ]
+
+    def forward_second(w, i):
+        slot, _, two = w
+        return [
+            push(slot(i, 3).at[up], slot(i, 2).at[up], two(1)),
+            push(slot(i, 1).at[low], slot(i, 2).at[low], two(-1)),
+        ]
+
+    share = [pl.ds(first + j * SHARE, SHARE) for j in range(4)]
+
+    def share_out(w, i, k):
+        slot = w[0]
+        return [
+            push(slot(i, k).at[share[0]], slot(i, k).at[share[1]], column(1)),
+            push(slot(i, k).at[share[0]], slot(i, k).at[share[2]], column(-1)),
+        ]
+
+    def share_on(w, i, k):
+        slot = w[0]
+        if (i + k) % 2 == 0:
+            return push(slot(i, k).at[share[1]], slot(i, k).at[share[3]], column(1))
+        return push(slot(i, k).at[share[2]], slot(i, k).at[share[3]], column(-1))
+
+    def arrived(copies):
+        for copy in copies:
+            copy.wait_recv()
+
+    for copy in own:
+        copy.wait()
+    table = {}
+    for n, w in enumerate(weights):
+        table["s1", n] = send_first(w)
+    for n, w in enumerate(weights):
+        table["s2", n, 0] = send_second(w, 0)
+
+    passing = []
+
+    def spread(slots):
+        for n, i, k in slots:
+            passing.append((n, i, k, share_out(weights[n], i, k)))
+
+    final = []
+
+    def pass_on(count):
+        for _ in range(min(count, len(passing))):
+            n, i, k, copies = passing.pop(0)
+            arrived(copies)
+            final.append(share_on(weights[n], i, k))
+
+    def service_first():
+        for n in (0, 1):
+            arrived(table["s1", n])
+        for n in (0, 1):
+            table["f1", n] = forward_first(weights[n])
+        for n in (0, 1):
+            for i in (1, 3):
+                table["s2", n, i] = send_second(weights[n], i)
+        spread([(n, i, 0) for n in (0, 1) for i in (1, 3)])
+
+    def service_second(i):
+        for n in (0, 1):
+            arrived(table["s2", n, i])
+            table["f2", n, i] = forward_second(weights[n], i)
+        spread([(n, i, k) for n in (0, 1) for k in (1, 3)])
+
+    def service_across():
+        for n in (0, 1):
+            arrived(table["f1", n])
+            table["s2", n, 2] = send_second(weights[n], 2)
+        spread([(n, 2, 0) for n in (0, 1)])
+
+    def service_last(i):
+        for n in (0, 1):
+            arrived(table["f2", n, i])
+        spread([(n, i, 2) for n in (0, 1)])
+
+    def norm_rows(read, write, i):
+        def body(t, carry):
+            at = pl.ds(pl.multiple_of(t * 32, 32), 32)
+            value = read(at)
+            mean = jnp.mean(value, axis=-1, keepdims=True)
+            centered = value - mean
+            variance = jnp.mean(centered * centered, axis=-1, keepdims=True)
+            write(at, centered * lax.rsqrt(variance + EPS) * gain[i : i + 1, :] + bias[i : i + 1, :])
+            return carry
+
+        lax.fori_loop(0, rows_here // 32, body, 0)
+
+    def write_acts(at, value):
+        acts[at, :] = value.astype(jnp.bfloat16)
+
+    norm_rows(lambda at: tokens[at, :].astype(jnp.float32), write_acts, 0)
+    seg_f = jnp.broadcast_to(seg[...].astype(jnp.float32), (rows_here, rows_here))
+    maskb[...] = jnp.where(seg_f == seg_f.T, 0.0, -jnp.inf)
+    joint[:, parts * chunk :] = jnp.zeros((rows_here, joint.shape[1] - parts * chunk), jnp.bfloat16)
+    att[...] = jnp.zeros_like(att)
+
+    def project(j, carry):
+        cols = pl.ds(pl.multiple_of(j * chunk, chunk), chunk)
+        pltpu.make_async_copy(wq_hbm.at[:, cols], wq.at[:, cols], local.at[first_wq + j]).wait()
+        value = jnp.dot(acts[0:rows_here, :], wq[:, cols], preferred_element_type=jnp.float32)
+        joint[:, cols] = (value + bq[:, cols]).astype(jnp.bfloat16)
+        return carry
+
+    lax.fori_loop(0, parts, project, 0)
+    service_first()
+
+    contract = (((1,), (1,)), ((), ()))
+
+    def head(h, carry):
+        start = (h * HEAD) // 128 * 128
+        lead = h * HEAD - start
+        lane = lax.broadcasted_iota(jnp.int32, (1, 256), 1)
+        inside = (lane >= lead) & (lane < lead + HEAD)
+        q = joint[:, pl.ds(pl.multiple_of(start, 128), 256)]
+        k = joint[:, pl.ds(pl.multiple_of(features + start, 128), 256)]
+        v = joint[:, pl.ds(pl.multiple_of(2 * features + start, 128), 256)]
+        zero = jnp.zeros_like(k)
+        k = jnp.where(inside, k, zero)
+        v = jnp.where(inside, v, zero)
+        scores = lax.dot_general(q, k, contract, preferred_element_type=jnp.float32)
+        scores = scores / math.sqrt(HEAD) + maskb[...]
+        top = jnp.max(scores, axis=-1, keepdims=True)
+        weights_ = jnp.exp(scores - top)
+        total = jnp.sum(weights_, axis=-1, keepdims=True)
+        soft = (weights_ * (1.0 / total)).astype(jnp.bfloat16)
+        mixed = jnp.dot(soft, v, preferred_element_type=jnp.float32)
+        into = pl.ds(pl.multiple_of(start, 128), 256)
+        att[:, into] = att[:, into] + mixed.astype(jnp.bfloat16)
+        return carry
+
+    lax.fori_loop(0, 8, head, 0)
+    service_second(0)
+    pass_on(4)
+    lax.fori_loop(8, 16, head, 0)
+    service_across()
+    pass_on(4)
+
+    wo_copy.wait()
+    for start, width in ((0, 512), (512, 512), (1024, 384)):
+        cols = slice(start, start + width)
+        value = jnp.dot(att[:, 0:features], wo[:, cols], preferred_element_type=jnp.float32)
+        resid[:, cols] = tokens[:, cols].astype(jnp.float32) + value
+    norm_rows(lambda at: resid[at, :], write_acts, 1)
+    swap = push(acts.at[pl.ds(0, rows_here)], acts.at[pl.ds(rows_here, rows_here)], partner)
+    service_second(1)
+    pass_on(4)
+    acc[...] = jnp.zeros_like(acc)
+    swap.wait_recv()
+
+    def ffn(slots):
+        def body(t, carry):
+            code = jnp.int32(0)
+            for n, (i, k) in enumerate(slots):
+                code = jnp.where(t == n, jnp.int32(i * 4 + k), code)
+            i, k = code // 4, code % 4
+            pre = lax.dot_general(acts[...], wa[k, i], contract, preferred_element_type=jnp.float32)
+            hidden = (0.5 * pre * (1.0 + lax.erf(pre * math.sqrt(0.5)))).astype(jnp.bfloat16)
+            for start, width in ((0, 512), (512, 512), (1024, 384)):
+                acc[:, start : start + width] += jnp.dot(
+                    hidden, wb[k, i, :, start : start + width], preferred_element_type=jnp.float32
+                )
+            return carry
+
+        lax.fori_loop(0, len(slots), body, 0)
+
+    done_final = [0]
+
+    def finish_shares():
+        pass_on(len(passing))
+        arrived(final[done_final[0] :])
+        done_final[0] = len(final)
+
+    service_second(3)
+    service_last(0)
+    pass_on(12)
+    service_second(2)
+    arrived(final)
+    done_final[0] = len(final)
+    ffn([(0, 0), (1, 0), (3, 0), (0, 1), (0, 3), (2, 0), (0, 2)])
+    service_last(1)
+    pass_on(10)
+    service_last(3)
+    pass_on(2)
+    arrived(final[done_final[0] :])
+    done_final[0] = len(final)
+    ffn([(1, 1), (1, 3), (3, 1), (3, 3)])
+    service_last(2)
+    finish_shares()
+    ffn([(1, 2), (2, 1), (3, 2), (2, 3), (2, 2)])
+
+    def narrow(t, carry):
+        at = pl.multiple_of(t * 32, 32)
+        psend[pl.ds(at, 32), :] = acc[pl.ds(rows_here + at, 32), :].astype(jnp.bfloat16)
+        return carry
+
+    lax.fori_loop(0, rows_here // 32, narrow, 0)
+    back = push(psend, precv, partner)
+    back.wait_recv()
+
+    def write_att(at, value):
+        att[at, 0:features] = value.astype(jnp.bfloat16)
+
+    norm_rows(
+        lambda at: resid[at, :] + (acc[at, :] + precv[at, :].astype(jnp.float32)), write_att, 2
+    )
+    for q in range(4):
+        place = lax.broadcasted_iota(jnp.int32, (MERGED_DEV, rows_here), 1)
+        pick = (idx[:, q : q + 1] == place).astype(jnp.bfloat16)
+        merged_out[:, q * features : (q + 1) * features] = jnp.dot(
+            pick, att[:, 0:features], preferred_element_type=jnp.float32
+        ).astype(jnp.bfloat16)
+    for copy in sent:
+        copy.wait_send()
+
+
+def layer(tokens, gain, bias, wq, bq, wo, wa, wb, seg, idx):
+    rows_here, features = tokens.shape
+    vmem = pl.BlockSpec(memory_space=pltpu.VMEM)
+    hbm = pl.BlockSpec(memory_space=pl.ANY)
+    copies = 2 * (2 + 2 + 16) + 90 + 2
+    return pl.pallas_call(
+        layer_kernel,
+        out_shape=jax.ShapeDtypeStruct((MERGED_DEV, 4 * features), jnp.bfloat16),
+        in_specs=[vmem, vmem, vmem, hbm, vmem, hbm, hbm, hbm, vmem, vmem],
+        out_specs=vmem,
+        scratch_shapes=[
+            pltpu.VMEM((4, 4, SLOT, features), jnp.bfloat16),
+            pltpu.VMEM((4, 4, SLOT, features), jnp.bfloat16),
+            pltpu.VMEM((features, 3 * features), jnp.bfloat16),
+            pltpu.VMEM((features, features), jnp.bfloat16),
+            pltpu.VMEM((rows_here, 3 * features + 128), jnp.bfloat16),
+            pltpu.VMEM((2 * rows_here, features), jnp.bfloat16),
+            pltpu.VMEM((rows_here, features), jnp.float32),
+            pltpu.VMEM((2 * rows_here, features), jnp.float32),
+            pltpu.VMEM((rows_here, features + 128), jnp.bfloat16),
+            pltpu.VMEM((rows_here, rows_here), jnp.float32),
+            pltpu.VMEM((rows_here, features), jnp.bfloat16),
+            pltpu.VMEM((rows_here, features), jnp.bfloat16),
+            pltpu.SemaphoreType.DMA((copies,)),
+            pltpu.SemaphoreType.DMA((copies,)),
+            pltpu.SemaphoreType.DMA((22,)),
+        ],
+        compiler_params=pltpu.CompilerParams(
+            collective_id=1, has_side_effects=True, vmem_limit_bytes=60 * 1024 * 1024
+        ),
+        name="layer",
+    )(tokens, gain, bias, wq, bq, wo, wa, wb, seg, idx)
 
 
 def per_device(
@@ -86,51 +436,21 @@
     n_rows = lax.axis_size("rows")
     n_mlp = lax.axis_size("mlp")
     member = lax.axis_index("mlp")
-    residual_in = tokens.astype(jnp.float32)
-    normed_in = layer_norm(residual_in, norm_gain[0], norm_bias[0]).astype(jnp.bfloat16)
-    joint = (
-        jnp.dot(normed_in, input_weight, preferred_element_type=jnp.float32) + input_bias
-    ).astype(jnp.bfloat16)
-    queries = joint[:, :features].reshape(rows_here, HEADS, HEAD)
-    keys_all = joint[:, features : 2 * features].reshape(rows_here, HEADS, HEAD)
-    values_all = joint[:, 2 * features :].reshape(rows_here, HEADS, HEAD)
-    scores = jnp.einsum(
-        "thd,uhd->htu", queries, keys_all, preferred_element_type=jnp.float32
-    ) / math.sqrt(HEAD)
-    allowed = segments[:, None] == segments[None, :]
-    scores = jnp.where(allowed[None], scores, -jnp.inf)
-    row_max = jnp.max(scores, axis=-1, keepdims=True)
-    weights = jnp.exp(scores - row_max)
-    softmax_out = (weights / jnp.sum(weights, axis=-1, keepdims=True)).astype(jnp.bfloat16)
-    attended = jnp.einsum(
-        "htu,uhd->thd", softmax_out, values_all, preferred_element_type=jnp.float32
-    )
-    attended = attended.astype(jnp.bfloat16).reshape(rows_here, features)
-    residual_mid = residual_in + jnp.dot(
-        attended, output_weight, preferred_element_type=jnp.float32
-    )
-    normed_mid = layer_norm(residual_mid, norm_gain[1], norm_bias[1]).astype(jnp.bfloat16)
-    contract = (((1,), (1,)), ((), ()))
-    pre_act = lax.dot_general(
-        normed_mid,
-        lax.all_gather(expand_weight, "rows", axis=0, tiled=True),
-        contract,
-        preferred_element_type=jnp.float32,
-    )
-    hidden = jax.nn.gelu(pre_act, approximate=False).astype(jnp.bfloat16)
-    unit_out = jnp.dot(
-        hidden,
-        lax.all_gather(reduce_weight, "rows", axis=0, tiled=True),
-        preferred_element_type=jnp.float32,
-    )
-    residual_out = residual_mid + unit_out
-    normed_out = layer_norm(residual_out, norm_gain[2], norm_bias[2]).astype(jnp.bfloat16)
     own_grid = lax.dynamic_slice_in_dim(grid_sides, member * REQ_DEV, REQ_DEV, 0)
     token_index, is_valid, owner_slot, own_counts = merge_layout(own_grid)
-    picked = jnp.take(normed_out, token_index.reshape(-1), axis=0).reshape(
-        token_index.shape[0], 4 * features
-    )
-    merged = jnp.where(is_valid[:, None], picked, jnp.zeros_like(picked))
+    token_index = jnp.where(is_valid[:, None], token_index, -1)
+    merged = layer(
+        tokens,
+        norm_gain,
+        norm_bias,
+        input_weight,
+        input_bias[None, :],
+        output_weight,
+        expand_weight,
+        reduce_weight,
+        segments[None, :],
+        token_index,
+    )
     projected = jnp.dot(
         lax.all_gather(merged, "mlp", axis=0, tiled=True),
         merger_weight,

time: 371 us -> 229 us (0.62)
  waiting for transfers between devices: 267 us -> 51.5 us
  Pallas kernels: 0 us -> 124 us
  matrix products: 51.2 us -> 8.93 us
  other arithmetic: 6.35 us -> 2.36 us
    all_gather x2 -> x0, waiting for transfers between devices: 211 us -> none  [the longest x1 116 us: per_device(): lax.all_gather(reduce_weight, 'rows', axis=0, tiled=True)]
    pallas_call x0 -> x1, Pallas kernels: none -> 124 us  [layer(): pl.pallas_call(layer_kernel, out_shape=jax.ShapeDtypeStruct((MERGED_DEV,...]
    dot_general x4 -> x0, matrix products: 38.7 us -> none  [the longest x1 26.1 us: per_device(): jnp.dot(hidden, lax.all_gather(reduce_weight, 'rows', axis=0, tiled=True)...]
  transfers between devices with their start and end apart: 4 -> 2, of which waited for: 4 -> 2; matrix products, arithmetic and copies ran while one was open for 7% -> 1% of each run, Pallas kernels for 0% -> 0%
where the time goes in v1:
time: 229 us
  Pallas kernels  124 us (54%)
  waiting for transfers between devices  51.5 us (22%)
  between operations  14.8 us (6%)
  blocking collectives  12 us (5%)
  matrix products  8.93 us (4%)
  starting transfers between devices  7.79 us (3%)
  local copies, waits for them, and re-layouts  7.63 us (3%)
  other arithmetic  2.36 us (1%)
    pallas_call x1, Pallas kernels, layer(): pl.pallas_call(layer_kernel, out_shape=jax.ShapeDtypeStruct((MERGED_DEV,...  124 us
    all_gather x1, waiting for transfers between devices, per_device(): lax.all_gather(merged, 'mlp', axis=0, tiled=True)  33 us
    all_to_all x1, waiting for transfers between devices, per_device(): lax.all_to_all(outgoing, ('rows', 'mlp'), split_axis=1, concat_axis=2, ti...  18.4 us
    unnamed x1, blocking collectives  12 us
    dot_general x1, matrix products, per_device(): jnp.dot(lax.all_gather(merged, 'mlp', axis=0, tiled=True), merger_weight,...  8.11 us
    all_to_all x1, starting transfers between devices, per_device(): lax.all_to_all(outgoing, ('rows', 'mlp'), split_axis=1, concat_axis=2, ti...  7.75 us
  transfers between devices with their start and end apart: 2, of which 2 were waited for; matrix products, arithmetic and copies ran while one was open for 1% of the time, Pallas kernels for 0%

profile of v1, /device:TPU:1, one launch (start us, length us, event | category | flops | bytes accessed | tf_op | source)
XLA Modules:
  0.0 229.0 jit_solution(14793782952599016791)
XLA Ops:
  7.2 0.8 constant_dynamic-slice_fusion
  8.0 0.2 reduce-window.15
  8.2 0.2 reduce-window.16
  8.4 0.1 convert_reduce_fusion.2
  8.5 0.2 select_reduce_fusion.5
  8.7 0.1 broadcast_add_fusion.1
  8.8 0.1 copy.54
  8.9 0.7 broadcast_select_fusion.idx
  9.6 1.3 broadcast_in_dim.83.bq
  11.0 123.8 %layer.1 = bf16[64,5632]{1,0:T(8,128)(2,1)} custom-call(bf16[256,1408]{1,0:T(8,128)(2,1)} %tokens.1, f32[3,1408]{1,0:T(4,128)} %gain.1, f32[3,1408]{1,0:T(4,128)} %bias.1, bf16[1408,4224]{1,0:T(8,128)(2,1)} %wq_hbm.1, f32[1,4224]{1,0:T(1,128)} %broadcast_in_dim.83.bq, bf16[1408,1408]{1,0:T(8,128)(2,1)} %wo_hbm.1, bf16[384,1408]{1,0:T(8,128)(2,1)} %wa_hbm.1, ...), custom_call_target="tpu_custom_call" | custom-call | tf_op jit(solution)/shard_map/layer/pallas_call | solution.py:390
  134.9 0.1 copy.55
  135.0 0.1 squeeze.50
  135.1 0.1 copy.56
  135.2 0.1 squeeze.51
  135.6 0.6 dynamic-slice
  136.8 0.2 convert_reduce_fusion
  137.1 33.0 %all-gather.4.cloned.1.call-done = bf16[512,5632]{1,0:T(8,128)(2,1)} async-done(((bf16[64,5632]{1,0:T(8,128)(2,1)}), bf16[512,5632]{1,0:T(8,128)(2,1)}) %all-gather.4.cloned.1.call-update) | async-done | bytes 5767184 | tf_op jit(solution)/shard_map/all_gather | solution.py:455
  170.1 8.1 %multiply_reduce_fusion.1 = (f32[512]{0:T(512)S(1)}, f32[512]{0:T(512)S(1)}, f32[512,512]{0,1:T(8,128)S(1)}) fusion(f32[512]{0:T(512)S(1)} %copy-done.2, bf16[512,5632]{1,0:T(8,128)(2,1)} %all-gather.4.cloned.1.call-done, bf16[5632,512]{1,0:T(8,128)(2,1)} %param.23), kind=kOutput, calls=%fused_computation.11 | convolution fusion | flops 2953837568 | bytes 12589056 | tf_op jit(solution)/shard_map/dot_general | solution.py:454
  178.2 0.1 select_reduce_fusion.1
  178.3 0.2 dynamic-update-slice.1
  178.6 0.2 dynamic-update-slice
  178.8 12.0 %all-reduce.2 = (f32[256]{0:T(256)S(1)}, f32[256]{0:T(256)S(1)}) all-reduce(f32[256]{0:T(256)S(1)} %dynamic-update-slice, f32[256]{0:T(256)S(1)} %dynamic-update-slice.1), channel_id=2, replica_groups=mesh['rows'=16,'mlp'=8] {'mlp'}, use_global_device_ids=true, to_apply=%add | all-reduce | flops 512 | bytes 4096
  190.8 0.1 reshape.409
  191.0 0.2 while.17
  191.2 0.1 select_reduce_fusion
  191.3 0.8 fusion.1
  192.2 1.5 copy.57
  193.7 7.7 %all-to-all-start = ((bf16[8,128,512]{2,0,1:T(8,128)(2,1)}), bf16[8,128,512]{2,0,1:T(8,128)(2,1)S(1)}, u32[]{:S(2)}, u32[]{:S(2)}) async-start(bf16[8,128,512]{2,0,1:T(8,128)(2,1)} %copy.57), calls=%async_computation | async-start | bytes 2097152 | tf_op jit(solution)/shard_map/all_to_all | solution.py:491
  201.5 0.6 dynamic_slice.36
  202.1 18.4 %all-to-all-done = bf16[8,128,512]{2,0,1:T(8,128)(2,1)S(1)} async-done(((bf16[8,128,512]{2,0,1:T(8,128)(2,1)}), bf16[8,128,512]{2,0,1:T(8,128)(2,1)S(1)}, u32[]{:S(2)}, u32[]{:S(2)}) %all-to-all-start) | async-done | bytes 1048608 | tf_op jit(solution)/shard_map/all_to_all | solution.py:491
  220.5 0.3 copy.58
  220.8 1.3 reshape.408
  (37 shorter events, 0.7 us)
Async XLA Ops:
  7.2 162.9 %all-gather.4.cloned.1.call-start = ((), (), s32[]{:S(2)}) async-start(), calls=%async_computation.1 | async-start | bytes 6488064 | tf_op jit(solution)/shard_map/all_gather | solution.py:455
  11.0 123.9 %copy-start.1 = (s32[32,2]{0,1:T(2,128)S(1)}, s32[32,2]{0,1:T(2,128)}, u32[]{:S(2)}) copy-start(s32[32,2]{0,1:T(2,128)} %param.26) | copy-start | bytes 772
  11.0 124.6 %copy-start.3 = (u32[128]{0:T(128)S(1)}, u32[128]{0:T(128)}, u32[]{:S(2)}) copy-start(u32[128]{0:T(128)} %constant.138) | copy-start | bytes 1540
  11.0 125.8 %copy-start = (s32[512,1]{0,1:T(1,128)S(1)}, s32[512,1]{0,1:T(1,128)}, u32[]{:S(2)}) copy-start(s32[512,1]{0,1:T(1,128)} %param.27) | copy-start | bytes 6148
  11.0 159.1 %copy-start.2 = (f32[512]{0:T(512)S(1)}, f32[512]{0:T(512)}, u32[]{:S(2)}) copy-start(f32[512]{0:T(512)} %param.24) | copy-start | bytes 6148
  193.7 26.8 %all-to-all-start = ((bf16[8,128,512]{2,0,1:T(8,128)(2,1)}), bf16[8,128,512]{2,0,1:T(8,128)(2,1)S(1)}, u32[]{:S(2)}, u32[]{:S(2)}) async-start(bf16[8,128,512]{2,0,1:T(8,128)(2,1)} %copy.57), calls=%async_computation | async-start | bytes 2097152 | tf_op jit(solution)/shard_map/all_to_all | solution.py:491
Sparse Core Ops, SparseCore 0:
  135.0 35.0 all-gather.3

commit v2 on v1

--- a/solution.py
+++ b/solution.py
@@ -15,17 +15,6 @@
 
 
 EPS = 1e-06
-
-
-def combined_all(part, axis, combine):
-    gathered = jax.tree.map(lambda a: lax.all_gather(a, axis), part)
-
-    def take(source):
-        return jax.tree.map(lambda a: lax.dynamic_index_in_dim(a, source, 0, False), gathered)
-
-    return lax.fori_loop(
-        1, lax.axis_size(axis), lambda source, state: combine(state, take(source)), take(0)
-    )
 
 
 def merge_layout(grid_block):
@@ -55,10 +44,6 @@
     )
     token_index = jnp.where(is_valid[:, None], token_index, 0)
     return (token_index, is_valid, owner_slot, counts)
-
-
-def combine_totals(earlier, latter):
-    return (earlier[0] + latter[0], jnp.maximum(earlier[1], latter[1]))
 
 
 MESH = pl.DeviceIdType.MESH
@@ -416,6 +401,199 @@
     )(tokens, gain, bias, wq, bq, wo, wa, wb, seg, idx)
 
 
+def merger_kernel(
+    merged, w_hbm, gain, req, counts, routes, outgoing, peaks,
+    blocks, weight, acc, scaled, stats, gathered, send, recv, local,
+):
+    row = lax.axis_index("rows")
+    member = lax.axis_index("mlp")
+    y, core = member // 2, member % 2
+    parts = 4
+    depth = w_hbm.shape[0] // parts
+    group = 8 * MERGED_DEV
+
+    def at_y(dy, other=False):
+        side = 1 - core if other else core
+        return ((y + dy + 4) % 4) * 2 + side
+
+    started = []
+    for q in range(parts):
+        copy = pltpu.make_async_copy(
+            merged.at[:, pl.ds(q * depth, depth)], blocks.at[q, member], local.at[q]
+        )
+        copy.start()
+        started.append(copy)
+    fetched = []
+    for q in range(parts):
+        rows_q = pl.ds(q * depth, depth)
+        copy = pltpu.make_async_copy(w_hbm.at[rows_q], weight.at[rows_q], local.at[parts + q])
+        copy.start()
+        fetched.append(copy)
+
+    barrier = pltpu.get_barrier_semaphore()
+    for step in range(1, 8):
+        pl.semaphore_signal(
+            barrier, inc=1, device_id=(row, (member + step) % 8), device_id_type=MESH
+        )
+    pl.semaphore_wait(barrier, 7)
+
+    sent = []
+
+    def push(src, dst, to):
+        k = len(sent)
+        copy = pltpu.make_async_remote_copy(
+            src_ref=src, dst_ref=dst, send_sem=send.at[k], recv_sem=recv.at[k],
+            device_id=(row, to), device_id_type=MESH,
+        )
+        copy.start()
+        sent.append(copy)
+        return copy
+
+    half = MERGED_DEV // 2
+    up, low = pl.ds(0, half), pl.ds(half, half)
+    first = []
+    for q in range(parts):
+        started[q].wait()
+        mine = blocks.at[q, member]
+        first.append([push(mine, mine, at_y(1)), push(mine, mine, at_y(-1))])
+    swap = []
+    for q in range(parts):
+        mine = blocks.at[q, member]
+        swap.append([push(mine, mine, at_y(0, True))])
+
+    wide = jnp.broadcast_to(routes[...].astype(jnp.float32), (group, 128))
+    target_row = wide.T[0:1, :].astype(jnp.int32)
+    rank = jnp.zeros((1, group), jnp.int32)
+    for t in range(4):
+        here = lax.broadcasted_iota(jnp.int32, (128, group), 0) + 128 * t
+        there = lax.broadcasted_iota(jnp.int32, (128, group), 1)
+        same = (routes[128 * t : 128 * (t + 1), :] == target_row) & (here < there)
+        rank = rank + jnp.sum(jnp.where(same, 1, 0), axis=0, keepdims=True)
+    key = target_row * 8 + rank
+
+    across = []
+    for q in range(parts + 1):
+        if q < parts:
+            below = blocks.at[q, at_y(-1)]
+            above = blocks.at[q, at_y(1)]
+            first[q][0].wait_recv()
+            across_q = [push(below.at[up], below.at[up], at_y(1))]
+            swap[q].append(push(below, below, at_y(0, True)))
+            first[q][1].wait_recv()
+            across_q.append(push(above.at[low], above.at[low], at_y(-1)))
+            swap[q].append(push(above, above, at_y(0, True)))
+            across.append(across_q)
+        if q >= 1:
+            p = q - 1
+            far = blocks.at[p, at_y(2)]
+            across[p][0].wait_recv()
+            across[p][1].wait_recv()
+            swap[p].append(push(far, far, at_y(0, True)))
+            fetched[p].wait()
+            for copy in swap[p]:
+                copy.wait_recv()
+
+            def column(n, carry, p=p):
+                cols = pl.ds(pl.multiple_of(n * 256, 256), 256)
+                value = jnp.dot(
+                    blocks[p].reshape(group, depth),
+                    weight[p * depth : (p + 1) * depth, cols],
+                    preferred_element_type=jnp.float32,
+                )
+                if p == 0:
+                    acc[:, cols] = value
+                else:
+                    acc[:, cols] += value
+                return carry
+
+            lax.fori_loop(0, acc.shape[1] // 256, column, 0)
+
+    lane = lax.broadcasted_iota(jnp.int32, (MERGED_DEV, 128), 1)
+
+    def tally(t, carry):
+        sums, tops = carry
+        at = pl.ds(pl.multiple_of(t * MERGED_DEV, MERGED_DEV), MERGED_DEV)
+        value = acc[at, :]
+        squares = jnp.sum(value * value, axis=1, keepdims=True)
+        top = jnp.max(value * gain[...], axis=1, keepdims=True)
+        owns = req[at, :] == lane
+        sums = sums + jnp.sum(jnp.where(owns, squares, 0.0), axis=0, keepdims=True)
+        tops = jnp.maximum(tops, jnp.max(jnp.where(owns, top, -jnp.inf), axis=0, keepdims=True))
+        return sums, tops
+
+    sums, tops = lax.fori_loop(
+        0, 8, tally, (jnp.zeros((1, 128), jnp.float32), jnp.full((1, 128), -jnp.inf, jnp.float32))
+    )
+    place = lax.broadcasted_iota(jnp.int32, (8, 128), 0)
+    both = jnp.where(place == 0, sums, tops)
+    stats[...] = both
+    gathered[member] = both
+    told = [push(stats, gathered.at[member], (member + step) % 8) for step in range(1, 8)]
+    for copy in told:
+        copy.wait_recv()
+    total = gathered[0, 0:1, :]
+    top = gathered[0, 1:2, :]
+    for m in range(1, 8):
+        total = total + gathered[m, 0:1, :]
+        top = jnp.maximum(top, gathered[m, 1:2, :])
+    number = counts[...]
+    inv_rms = lax.rsqrt(total / (jnp.maximum(number, 1.0) * OUT) + EPS)
+    peaks[...] = jnp.where(number > 0.0, top * inv_rms, 0.0)
+
+    def scale(t, carry):
+        at = pl.ds(pl.multiple_of(t * MERGED_DEV, MERGED_DEV), MERGED_DEV)
+        row_inv = jnp.sum(jnp.where(req[at, :] == lane, inv_rms, 0.0), axis=1, keepdims=True)
+        scaled[at, :] = (acc[at, :] * gain[...] * row_inv).astype(jnp.bfloat16)
+        return carry
+
+    lax.fori_loop(0, 8, scale, 0)
+
+    def route(t, carry):
+        at = pl.multiple_of(t * 256, 256)
+        slot = lax.broadcasted_iota(jnp.int32, (256, group), 0) + at
+        pick = (slot == key).astype(jnp.bfloat16)
+        outgoing[pl.ds(at, 256), :] = jnp.dot(
+            pick, scaled[...], preferred_element_type=jnp.float32
+        ).astype(jnp.bfloat16)
+        return carry
+
+    lax.fori_loop(0, outgoing.shape[0] // 256, route, 0)
+    for copy in sent:
+        copy.wait_send()
+
+
+def merger(merged, weight, gain, req, counts, routes):
+    vmem = pl.BlockSpec(memory_space=pltpu.VMEM)
+    hbm = pl.BlockSpec(memory_space=pl.ANY)
+    depth, width = weight.shape
+    group = 8 * MERGED_DEV
+    copies = 32 + 7
+    return pl.pallas_call(
+        merger_kernel,
+        out_shape=(
+            jax.ShapeDtypeStruct((1024, width), jnp.bfloat16),
+            jax.ShapeDtypeStruct((1, 128), jnp.float32),
+        ),
+        in_specs=[hbm, hbm, vmem, vmem, vmem, vmem],
+        out_specs=(vmem, vmem),
+        scratch_shapes=[
+            pltpu.VMEM((4, 8, MERGED_DEV, depth // 4), jnp.bfloat16),
+            pltpu.VMEM((depth, width), jnp.bfloat16),
+            pltpu.VMEM((group, width), jnp.float32),
+            pltpu.VMEM((group, width), jnp.bfloat16),
+            pltpu.VMEM((8, 128), jnp.float32),
+            pltpu.VMEM((8, 8, 128), jnp.float32),
+            pltpu.SemaphoreType.DMA((copies,)),
+            pltpu.SemaphoreType.DMA((copies,)),
+            pltpu.SemaphoreType.DMA((8,)),
+        ],
+        compiler_params=pltpu.CompilerParams(
+            collective_id=2, has_side_effects=True, vmem_limit_bytes=60 * 1024 * 1024
+        ),
+        name="merger",
+    )(merged, weight, gain, req, counts, routes)
+
+
 def per_device(
     tokens,
     norm_gain,
@@ -431,8 +609,6 @@
     grid_sides,
     routes,
 ):
-    rows_here = tokens.shape[0]
-    features = tokens.shape[1]
     n_rows = lax.axis_size("rows")
     n_mlp = lax.axis_size("mlp")
     member = lax.axis_index("mlp")
@@ -451,45 +627,22 @@
         segments[None, :],
         token_index,
     )
-    projected = jnp.dot(
-        lax.all_gather(merged, "mlp", axis=0, tiled=True),
-        merger_weight,
-        preferred_element_type=jnp.float32,
-    )
-    group_index, group_valid, group_owner, group_counts = jax.vmap(merge_layout)(
+    group_valid, group_owner, group_counts = jax.vmap(merge_layout)(
         grid_sides.reshape(n_mlp, REQ_DEV, 2)
-    )
+    )[1:]
     group_requests = n_mlp * REQ_DEV
     member_base = (REQ_DEV * jnp.arange(n_mlp, dtype=jnp.int32))[:, None]
-    request_of_row = jnp.where(group_valid, group_owner + member_base, group_requests).reshape(-1)
-    counts = group_counts.reshape(-1)
-    gained = projected * output_gain
-    row_squares = jnp.sum(projected * projected, axis=1)
-    row_peaks = jnp.max(gained, axis=1)
-    member_of = jnp.arange(group_requests, dtype=jnp.int32)[:, None] == request_of_row[None, :]
-    sums_part = jnp.sum(jnp.where(member_of, row_squares[None, :], 0.0), axis=1)
-    peaks_part = jnp.max(jnp.where(member_of, row_peaks[None, :], -jnp.inf), axis=1)
-    square_sum, peak_all = combined_all((sums_part, peaks_part), "mlp", combine_totals)
-    inv_rms = lax.rsqrt(square_sum / (jnp.maximum(counts, 1).astype(jnp.float32) * OUT) + EPS)
-    row_inv = jnp.sum(jnp.where(member_of, inv_rms[:, None], 0.0), axis=0)
-    scaled = (gained * row_inv[:, None]).astype(jnp.bfloat16)
-    peak_values = jnp.where(counts > 0, peak_all * inv_rms, 0.0)
-    peaks_own = lax.dynamic_slice_in_dim(peak_values, member * REQ_DEV, REQ_DEV, 0)
-    targets = routes[:, 0]
-    group_rows = targets.shape[0]
-    row_order = jnp.arange(group_rows, dtype=jnp.int32)
-    same_target = (targets[:, None] == targets[None, :]) & (row_order[None, :] < row_order[:, None])
-    target_rank = jnp.sum(same_target.astype(jnp.int32), axis=1)
-    devices = n_rows * n_mlp
-    capacity = max(2, 2 * MERGED_DEV // n_rows)
-    slot_key = target_rank * devices + targets
-    selector = (
-        jnp.arange(capacity * devices, dtype=jnp.int32)[:, None] == slot_key[None, :]
-    ).astype(jnp.bfloat16)
-    outgoing = jnp.dot(selector, scaled, preferred_element_type=jnp.float32).astype(jnp.bfloat16)
-    outgoing = outgoing.reshape(capacity, devices, scaled.shape[1])
-    arrived = lax.all_to_all(outgoing, ("rows", "mlp"), split_axis=1, concat_axis=2, tiled=True)
-    delivered = arrived.reshape(capacity * n_rows, n_mlp * scaled.shape[1])
+    request_of_row = jnp.where(group_valid, group_owner + member_base, 128).reshape(-1, 1)
+    counts = jnp.pad(group_counts.reshape(1, -1).astype(jnp.float32), ((0, 0), (0, 128 - group_requests)))
+    outgoing, peak_values = merger(
+        merged, merger_weight, output_gain[None, :], request_of_row, counts, routes
+    )
+    peaks_own = lax.dynamic_slice_in_dim(peak_values[0], member * REQ_DEV, REQ_DEV, 0)
+    capacity = outgoing.shape[0] // (n_rows * n_mlp)
+    outgoing = outgoing.reshape(n_rows * n_mlp, capacity, -1)
+    arrived = lax.all_to_all(outgoing, ("rows", "mlp"), split_axis=0, concat_axis=0, tiled=True)
+    arrived = arrived.reshape(n_rows, n_mlp, capacity, -1)
+    delivered = arrived.transpose(2, 0, 1, 3).reshape(capacity * n_rows, -1)
     return (delivered, peaks_own)
 
 

time: 229 us -> 201 us (0.88)
  Pallas kernels: 124 us -> 167 us
  waiting for transfers between devices: 51.5 us -> 17.8 us
  between operations: 14.8 us -> 0.7 us
  blocking collectives: 12 us -> 0 us
  matrix products: 8.93 us -> 0 us
  starting transfers between devices: 7.79 us -> 4.58 us
    pallas_call x0 -> x1, Pallas kernels: none -> 43.2 us  [merger(): pl.pallas_call(merger_kernel, out_shape=(jax.ShapeDtypeStruct((1024, widt...]
    all_gather x1 -> x0, waiting for transfers between devices: 33 us -> none  [per_device(): lax.all_gather(merged, 'mlp', axis=0, tiled=True)]
    unnamed x1 -> x0, blocking collectives: 12 us -> none
    dot_general x2 -> x0, matrix products: 8.93 us -> none  [the longest x1 8.11 us: per_device(): jnp.dot(lax.all_gather(merged, 'mlp', axis=0, tiled=True), merger_weight,...]
    all_to_all x1, starting transfers between devices: 7.75 us -> 4.58 us  [per_device(): lax.all_to_all(outgoing, ('rows', 'mlp'), split_axis=0, concat_axis=0, ti...]
    reshape x2 -> x1, local copies, waits for them, and re-layouts: 2.86 us -> 0.31 us  [per_device(): arrived = arrived.reshape(n_rows, n_mlp, capacity, -1)]
  transfers between devices with their start and end apart: 2 -> 1, of which waited for: 2 -> 1; matrix products, arithmetic and copies ran while one was open for 1% -> 1% of each run, Pallas kernels for 0% -> 0%
where the time goes in v2:
time: 201 us
  Pallas kernels  167 us (83%)
  waiting for transfers between devices  17.8 us (9%)
  local copies, waits for them, and re-layouts  9.15 us (5%)
  starting transfers between devices  4.58 us (2%)
    pallas_call x1, Pallas kernels, layer(): pl.pallas_call(layer_kernel, out_shape=jax.ShapeDtypeStruct((MERGED_DEV,...  124 us
    pallas_call x1, Pallas kernels, merger(): pl.pallas_call(merger_kernel, out_shape=(jax.ShapeDtypeStruct((1024, widt...  43.2 us
    all_to_all x1, waiting for transfers between devices, per_device(): lax.all_to_all(outgoing, ('rows', 'mlp'), split_axis=0, concat_axis=0, ti...  17.8 us
    all_to_all x1, starting transfers between devices, per_device(): lax.all_to_all(outgoing, ('rows', 'mlp'), split_axis=0, concat_axis=0, ti...  4.58 us
  transfers between devices with their start and end apart: 1, of which 1 were waited for; matrix products, arithmetic and copies ran while one was open for 1% of the time, Pallas kernels for 0%

profile of v2, /device:TPU:1, one launch (start us, length us, event | category | flops | bytes accessed | tf_op | source)
XLA Modules:
  0.0 200.9 jit_solution(7619561023957932256)
XLA Ops:
  0.6 0.8 reshape.556
  1.4 0.1 squeeze.22
  1.5 0.1 copy.55
  1.6 0.1 squeeze.21
  1.6 0.1 copy.54
  1.7 0.8 constant_dynamic-slice_fusion
  2.5 0.2 reduce-window.15
  2.7 0.1 convert_reduce_fusion.1
  2.8 0.2 reduce-window.16
  3.0 0.2 select_reduce_fusion.2
  3.2 0.1 broadcast_add_fusion.1
  3.4 0.1 convert_reduce_fusion
  3.5 1.3 broadcast_in_dim.42.bq
  4.8 0.1 copy.53
  4.9 0.7 broadcast_select_fusion.idx
  5.6 0.1 add_select_fusion
  5.7 0.9 select_n.161.req
  6.6 1.5 copy.57.routes
  8.1 0.5 pad.4.counts
  8.7 123.8 %layer.1.merged = bf16[64,5632]{1,0:T(8,128)(2,1)} custom-call(bf16[256,1408]{1,0:T(8,128)(2,1)} %tokens.1, f32[3,1408]{1,0:T(4,128)} %gain.1, f32[3,1408]{1,0:T(4,128)} %bias.1, bf16[1408,4224]{1,0:T(8,128)(2,1)} %wq_hbm.1, f32[1,4224]{1,0:T(1,128)} %broadcast_in_dim.42.bq, bf16[1408,1408]{1,0:T(8,128)(2,1)} %wo_hbm.1, bf16[384,1408]{1,0:T(8,128)(2,1)} %wa_hbm.1, ...), custom_call_target="tpu_custom_call" | custom-call | tf_op jit(solution)/shard_map/layer/pallas_call | solution.py:375
  132.4 43.2 %merger.1 = (bf16[1024,512]{1,0:T(8,128)(2,1)}, f32[1,128]{1,0:T(1,128)}) custom-call(bf16[64,5632]{1,0:T(8,128)(2,1)} %layer.1.merged, bf16[5632,512]{1,0:T(8,128)(2,1)} %w_hbm.1, f32[1,512]{1,0:T(1,128)} %bitcast.104, s32[512,1]{1,0:T(8,128)} %select_n.161.req, f32[1,128]{1,0:T(1,128)} %pad.4.counts, s32[512,1]{1,0:T(8,128)} %copy.57.routes), custom_call_target="tpu_custom_call" | custom-call | tf_op jit(solution)/shard_map/merger/pallas_call | solution.py:571
  175.7 4.6 %all-to-all-start = ((bf16[128,8,512]{2,1,0:T(8,128)(2,1)}), bf16[128,8,512]{2,1,0:T(8,128)(2,1)S(1)}, u32[]{:S(2)}, u32[]{:S(2)}) async-start(bf16[128,8,512]{2,1,0:T(8,128)(2,1)} %bitcast.102), calls=%async_computation | async-start | bytes 2097152 | tf_op jit(solution)/shard_map/all_to_all | solution.py:643
  180.2 1.2 dynamic-slice_bitcast_fusion
  181.5 17.8 %all-to-all-done = bf16[128,8,512]{2,1,0:T(8,128)(2,1)S(1)} async-done(((bf16[128,8,512]{2,1,0:T(8,128)(2,1)}), bf16[128,8,512]{2,1,0:T(8,128)(2,1)S(1)}, u32[]{:S(2)}, u32[]{:S(2)}) %all-to-all-start) | async-done | bytes 1048608 | tf_op jit(solution)/shard_map/all_to_all | solution.py:643
  199.3 0.3 copy.58
  199.6 1.4 copy.70
  (10 shorter events, 0.1 us)
Async XLA Ops:
  175.7 23.6 %all-to-all-start = ((bf16[128,8,512]{2,1,0:T(8,128)(2,1)}), bf16[128,8,512]{2,1,0:T(8,128)(2,1)S(1)}, u32[]{:S(2)}, u32[]{:S(2)}) async-start(bf16[128,8,512]{2,1,0:T(8,128)(2,1)} %bitcast.102), calls=%async_computation | async-start | bytes 2097152 | tf_op jit(solution)/shard_map/all_to_all | solution.py:643

commit v3 on v2

--- a/solution.py
+++ b/solution.py
@@ -17,36 +17,21 @@
 EPS = 1e-06
 
 
-def merge_layout(grid_block):
-    heights = grid_block[:, 0]
-    widths_all = grid_block[:, 1]
-    lengths = jnp.where(heights > 0, 1 + heights * widths_all, 0)
-    starts = jnp.cumsum(lengths) - lengths
-    counts = heights // 2 * (widths_all // 2)
-    merge_starts = jnp.cumsum(counts) - counts
-    merge_ends = merge_starts + counts
-    merge_slots = jnp.arange(MERGED_DEV, dtype=jnp.int32)
-    owner_slot = jnp.sum((merge_ends[None, :] <= merge_slots[:, None]).astype(jnp.int32), axis=1)
-    is_valid = owner_slot < REQ_DEV
-    chosen = (owner_slot[:, None] == jnp.arange(REQ_DEV, dtype=jnp.int32)[None, :]).astype(
-        jnp.int32
-    )
-    row_width = jnp.sum(chosen * widths_all[None, :], axis=1)
-    row_start = jnp.sum(chosen * starts[None, :], axis=1)
-    row_merge = jnp.sum(chosen * merge_starts[None, :], axis=1)
-    within = merge_slots - row_merge
-    half_width = jnp.maximum(row_width // 2, 1)
-    patch_row = within // half_width
-    patch_col = within - patch_row * half_width
-    corner = row_start + 1 + 2 * patch_row * row_width + 2 * patch_col
-    token_index = jnp.stack(
-        [corner, corner + 1, corner + row_width, corner + row_width + 1], axis=1
-    )
-    token_index = jnp.where(is_valid[:, None], token_index, 0)
-    return (token_index, is_valid, owner_slot, counts)
-
-
 MESH = pl.DeviceIdType.MESH
+
+
+def request_spans(grid, first):
+    spans = []
+    token, merge = 0, 0
+    for k in range(REQ_DEV):
+        height, width = grid[first + k, 0], grid[first + k, 1]
+        count = lax.div(height, 2) * lax.div(width, 2)
+        spans.append((height, width, token, merge, count))
+        token = token + jnp.where(height > 0, 1 + height * width, 0)
+        merge = merge + count
+    return spans
+
+
 PLANE = 144
 HALF = 80
 SHARE = 16
@@ -54,14 +39,15 @@
 
 
 def layer_kernel(
-    tokens, gain, bias, wq_hbm, bq, wo_hbm, wa_hbm, wb_hbm, seg, idx, merged_out,
-    wa, wb, wq, wo, joint, acts, resid, acc, att, maskb, psend, precv,
+    tokens, gain, bias, wq_hbm, bq, wo_hbm, wa_hbm, wb_hbm, seg, grid, merged_out,
+    wa, wb, wq, wo, joint, acts, resid, acc, att, maskb, pick, psend, precv,
     send, recv, local,
 ):
     row = lax.axis_index("rows")
     member = lax.axis_index("mlp")
     x, z = row // 4, row % 4
     y, core = member // 2, member % 2
+    zero = row - row
     features = tokens.shape[1]
     rows_here = tokens.shape[0]
 
@@ -237,26 +223,49 @@
             write(at, centered * lax.rsqrt(variance + EPS) * gain[i : i + 1, :] + bias[i : i + 1, :])
             return carry
 
-        lax.fori_loop(0, rows_here // 32, body, 0)
+        lax.fori_loop(0, rows_here // 32, body, 0, unroll=2)
 
     def write_acts(at, value):
         acts[at, :] = value.astype(jnp.bfloat16)
 
     norm_rows(lambda at: tokens[at, :].astype(jnp.float32), write_acts, 0)
-    seg_f = jnp.broadcast_to(seg[...].astype(jnp.float32), (rows_here, rows_here))
+    seg_f = jnp.broadcast_to(
+        seg[...].astype(jnp.float32).reshape(1, rows_here), (rows_here, rows_here)
+    )
     maskb[...] = jnp.where(seg_f == seg_f.T, 0.0, -jnp.inf)
     joint[:, parts * chunk :] = jnp.zeros((rows_here, joint.shape[1] - parts * chunk), jnp.bfloat16)
     att[...] = jnp.zeros_like(att)
+
+    def pick_rows():
+        slot = lax.broadcasted_iota(jnp.int32, (MERGED_DEV, rows_here), 0)
+        place = lax.broadcasted_iota(jnp.int32, (MERGED_DEV, rows_here), 1)
+        corner = jnp.full((MERGED_DEV, rows_here), -1000, jnp.int32)
+        wide = jnp.zeros((MERGED_DEV, rows_here), jnp.int32)
+        for _, width, token, merge, count in request_spans(grid, member * REQ_DEV):
+            within = slot - merge
+            half = lax.div(width, 2)
+            line = jnp.zeros_like(within)
+            for n in range(1, 4):
+                line = line + jnp.where(within >= n * half, 1, 0)
+            at = token + 1 + 2 * line * width + 2 * (within - line * half)
+            here = (within >= 0) & (within < count)
+            corner = jnp.where(here, at, corner)
+            wide = jnp.where(here, width, wide)
+        one, none = jnp.ones((), jnp.float32), jnp.zeros((), jnp.float32)
+        for q in range(4):
+            at = corner + (q % 2) + (wide if q >= 2 else 0)
+            pick[q] = jnp.where(at == place, one, none).astype(jnp.bfloat16)
 
     def project(j, carry):
         cols = pl.ds(pl.multiple_of(j * chunk, chunk), chunk)
         pltpu.make_async_copy(wq_hbm.at[:, cols], wq.at[:, cols], local.at[first_wq + j]).wait()
         value = jnp.dot(acts[0:rows_here, :], wq[:, cols], preferred_element_type=jnp.float32)
-        joint[:, cols] = (value + bq[:, cols]).astype(jnp.bfloat16)
+        joint[:, cols] = (value + bq[cols].reshape(1, chunk)).astype(jnp.bfloat16)
         return carry
 
     lax.fori_loop(0, parts, project, 0)
     service_first()
+    pick_rows()
 
     contract = (((1,), (1,)), ((), ()))
 
@@ -282,10 +291,11 @@
         att[:, into] = att[:, into] + mixed.astype(jnp.bfloat16)
         return carry
 
-    lax.fori_loop(0, 8, head, 0)
+    lax.fori_loop(0, 6, head, 0, unroll=2)
+    pass_on(4)
+    lax.fori_loop(6, 10, head, 0, unroll=2)
     service_second(0)
-    pass_on(4)
-    lax.fori_loop(8, 16, head, 0)
+    lax.fori_loop(10, 16, head, 0, unroll=2)
     service_across()
     pass_on(4)
 
@@ -296,51 +306,90 @@
         resid[:, cols] = tokens[:, cols].astype(jnp.float32) + value
     norm_rows(lambda at: resid[at, :], write_acts, 1)
     swap = push(acts.at[pl.ds(0, rows_here)], acts.at[pl.ds(rows_here, rows_here)], partner)
+    settled = [0]
+
+    def settle(count=None):
+        stop = len(final) if count is None else settled[0] + count
+        arrived(final[settled[0] : stop])
+        settled[0] = stop
+
     service_second(1)
-    pass_on(4)
+    pass_on(2)
+    settle(8)
     acc[...] = jnp.zeros_like(acc)
     swap.wait_recv()
 
-    def ffn(slots):
-        def body(t, carry):
-            code = jnp.int32(0)
-            for n, (i, k) in enumerate(slots):
-                code = jnp.where(t == n, jnp.int32(i * 4 + k), code)
-            i, k = code // 4, code % 4
-            pre = lax.dot_general(acts[...], wa[k, i], contract, preferred_element_type=jnp.float32)
-            hidden = (0.5 * pre * (1.0 + lax.erf(pre * math.sqrt(0.5)))).astype(jnp.bfloat16)
-            for start, width in ((0, 512), (512, 512), (1024, 384)):
-                acc[:, start : start + width] += jnp.dot(
-                    hidden, wb[k, i, :, start : start + width], preferred_element_type=jnp.float32
-                )
-            return carry
-
-        lax.fori_loop(0, len(slots), body, 0)
-
-    done_final = [0]
-
-    def finish_shares():
-        pass_on(len(passing))
-        arrived(final[done_final[0] :])
-        done_final[0] = len(final)
-
-    service_second(3)
-    service_last(0)
-    pass_on(12)
-    service_second(2)
-    arrived(final)
-    done_final[0] = len(final)
-    ffn([(0, 0), (1, 0), (3, 0), (0, 1), (0, 3), (2, 0), (0, 2)])
-    service_last(1)
-    pass_on(10)
-    service_last(3)
-    pass_on(2)
-    arrived(final[done_final[0] :])
-    done_final[0] = len(final)
-    ffn([(1, 1), (1, 3), (3, 1), (3, 3)])
-    service_last(2)
-    finish_shares()
-    ffn([(1, 2), (2, 1), (3, 2), (2, 3), (2, 2)])
+    def before_1():
+        pass_on(4)
+
+    def before_4():
+        settle()
+
+    def before_5():
+        service_second(3)
+
+    def before_6():
+        service_last(0)
+        pass_on(4)
+        settle()
+
+    def before_7():
+        pass_on(2)
+
+    def before_9():
+        settle()
+
+    def before_10():
+        service_second(2)
+
+    def before_11():
+        pass_on(4)
+        service_last(1)
+        pass_on(2)
+        settle()
+
+    def before_12():
+        service_last(3)
+
+    def before_13():
+        pass_on(2)
+        settle()
+
+    def before_14():
+        service_last(2)
+
+    def before_15():
+        pass_on(2)
+        settle()
+
+    order = [
+        (0, 0), (1, 0), (3, 0), (0, 1), (0, 3), (1, 1), (1, 3), (3, 1),
+        (3, 3), (2, 0), (0, 2), (1, 2), (2, 1), (3, 2), (2, 3), (2, 2),
+    ]
+    services = {
+        1: before_1, 4: before_4, 5: before_5, 6: before_6, 7: before_7, 9: before_9,
+        10: before_10, 11: before_11, 12: before_12, 13: before_13, 14: before_14, 15: before_15,
+    }
+
+    def ffn(t, carry):
+        code = zero
+        for n, (i, k) in enumerate(order):
+            code = jnp.where(t == n, i * 4 + k, code)
+        i, k = code // 4, code % 4
+        pre = lax.dot_general(acts[...], wa[k, i], contract, preferred_element_type=jnp.float32)
+        hidden = (0.5 * pre * (1.0 + lax.erf(pre * math.sqrt(0.5)))).astype(jnp.bfloat16)
+        for start, width in ((0, 512), (512, 512), (1024, 384)):
+            acc[:, start : start + width] += jnp.dot(
+                hidden, wb[k, i, :, start : start + width], preferred_element_type=jnp.float32
+            )
+        return carry
+
+    begun = 0
+    for n in [*sorted(services), len(order)]:
+        lax.fori_loop(begun, n, ffn, 0)
+        if n in services:
+            services[n]()
+        begun = n
 
     def narrow(t, carry):
         at = pl.multiple_of(t * 32, 32)
@@ -358,16 +407,14 @@
         lambda at: resid[at, :] + (acc[at, :] + precv[at, :].astype(jnp.float32)), write_att, 2
     )
     for q in range(4):
-        place = lax.broadcasted_iota(jnp.int32, (MERGED_DEV, rows_here), 1)
-        pick = (idx[:, q : q + 1] == place).astype(jnp.bfloat16)
         merged_out[:, q * features : (q + 1) * features] = jnp.dot(
-            pick, att[:, 0:features], preferred_element_type=jnp.float32
+            pick[q], att[:, 0:features], preferred_element_type=jnp.float32
         ).astype(jnp.bfloat16)
     for copy in sent:
         copy.wait_send()
 
 
-def layer(tokens, gain, bias, wq, bq, wo, wa, wb, seg, idx):
+def layer(tokens, gain, bias, wq, bq, wo, wa, wb, seg, grid):
     rows_here, features = tokens.shape
     vmem = pl.BlockSpec(memory_space=pltpu.VMEM)
     hbm = pl.BlockSpec(memory_space=pl.ANY)
@@ -375,7 +422,10 @@
     return pl.pallas_call(
         layer_kernel,
         out_shape=jax.ShapeDtypeStruct((MERGED_DEV, 4 * features), jnp.bfloat16),
-        in_specs=[vmem, vmem, vmem, hbm, vmem, hbm, hbm, hbm, vmem, vmem],
+        in_specs=[
+            vmem, vmem, vmem, hbm, vmem, hbm, hbm, hbm, vmem,
+            pl.BlockSpec(memory_space=pltpu.SMEM),
+        ],
         out_specs=vmem,
         scratch_shapes=[
             pltpu.VMEM((4, 4, SLOT, features), jnp.bfloat16),
@@ -388,6 +438,7 @@
             pltpu.VMEM((2 * rows_here, features), jnp.float32),
             pltpu.VMEM((rows_here, features + 128), jnp.bfloat16),
             pltpu.VMEM((rows_here, rows_here), jnp.float32),
+            pltpu.VMEM((4, MERGED_DEV, rows_here), jnp.bfloat16),
             pltpu.VMEM((rows_here, features), jnp.bfloat16),
             pltpu.VMEM((rows_here, features), jnp.bfloat16),
             pltpu.SemaphoreType.DMA((copies,)),
@@ -398,12 +449,12 @@
             collective_id=1, has_side_effects=True, vmem_limit_bytes=60 * 1024 * 1024
         ),
         name="layer",
-    )(tokens, gain, bias, wq, bq, wo, wa, wb, seg, idx)
+    )(tokens, gain, bias, wq, bq, wo, wa, wb, seg, grid)
 
 
 def merger_kernel(
-    merged, w_hbm, gain, req, counts, routes, outgoing, peaks,
-    blocks, weight, acc, scaled, stats, gathered, send, recv, local,
+    merged, w_hbm, gain, grid, routes, outgoing, peaks,
+    blocks, weight, acc, req, scaled, stats, gathered, send, recv, local,
 ):
     row = lax.axis_index("rows")
     member = lax.axis_index("mlp")
@@ -461,15 +512,27 @@
         mine = blocks.at[q, member]
         swap.append([push(mine, mine, at_y(0, True))])
 
-    wide = jnp.broadcast_to(routes[...].astype(jnp.float32), (group, 128))
-    target_row = wide.T[0:1, :].astype(jnp.int32)
+    target_row = routes[...]
+    target_col = jnp.broadcast_to(target_row.astype(jnp.float32), (128, group)).T.astype(jnp.int32)
     rank = jnp.zeros((1, group), jnp.int32)
     for t in range(4):
         here = lax.broadcasted_iota(jnp.int32, (128, group), 0) + 128 * t
         there = lax.broadcasted_iota(jnp.int32, (128, group), 1)
-        same = (routes[128 * t : 128 * (t + 1), :] == target_row) & (here < there)
+        same = (target_col[128 * t : 128 * (t + 1), 0:1] == target_row) & (here < there)
         rank = rank + jnp.sum(jnp.where(same, 1, 0), axis=0, keepdims=True)
     key = target_row * 8 + rank
+
+    lane_row = lax.broadcasted_iota(jnp.int32, (1, 128), 1)
+    number = jnp.zeros((1, 128), jnp.int32)
+    slot = lax.broadcasted_iota(jnp.int32, (MERGED_DEV, 128), 0)
+    for t in range(8):
+        owner = jnp.full((MERGED_DEV, 128), 128, jnp.int32)
+        for k, (_, _, _, merge, count) in enumerate(request_spans(grid, t * REQ_DEV)):
+            here = (slot >= merge) & (slot < merge + count)
+            owner = jnp.where(here, t * REQ_DEV + k, owner)
+            number = jnp.where(lane_row == t * REQ_DEV + k, count, number)
+        req[t * MERGED_DEV : (t + 1) * MERGED_DEV, :] = owner
+    number = number.astype(jnp.float32)
 
     across = []
     for q in range(parts + 1):
@@ -509,13 +572,14 @@
             lax.fori_loop(0, acc.shape[1] // 256, column, 0)
 
     lane = lax.broadcasted_iota(jnp.int32, (MERGED_DEV, 128), 1)
+    gain_row = gain[...].reshape(1, acc.shape[1])
 
     def tally(t, carry):
         sums, tops = carry
         at = pl.ds(pl.multiple_of(t * MERGED_DEV, MERGED_DEV), MERGED_DEV)
         value = acc[at, :]
         squares = jnp.sum(value * value, axis=1, keepdims=True)
-        top = jnp.max(value * gain[...], axis=1, keepdims=True)
+        top = jnp.max(value * gain_row, axis=1, keepdims=True)
         owns = req[at, :] == lane
         sums = sums + jnp.sum(jnp.where(owns, squares, 0.0), axis=0, keepdims=True)
         tops = jnp.maximum(tops, jnp.max(jnp.where(owns, top, -jnp.inf), axis=0, keepdims=True))
@@ -536,14 +600,13 @@
     for m in range(1, 8):
         total = total + gathered[m, 0:1, :]
         top = jnp.maximum(top, gathered[m, 1:2, :])
-    number = counts[...]
     inv_rms = lax.rsqrt(total / (jnp.maximum(number, 1.0) * OUT) + EPS)
     peaks[...] = jnp.where(number > 0.0, top * inv_rms, 0.0)
 
     def scale(t, carry):
         at = pl.ds(pl.multiple_of(t * MERGED_DEV, MERGED_DEV), MERGED_DEV)
         row_inv = jnp.sum(jnp.where(req[at, :] == lane, inv_rms, 0.0), axis=1, keepdims=True)
-        scaled[at, :] = (acc[at, :] * gain[...] * row_inv).astype(jnp.bfloat16)
+        scaled[at, :] = (acc[at, :] * gain_row * row_inv).astype(jnp.bfloat16)
         return carry
 
     lax.fori_loop(0, 8, scale, 0)
@@ -562,7 +625,7 @@
         copy.wait_send()
 
 
-def merger(merged, weight, gain, req, counts, routes):
+def merger(merged, weight, gain, grid, routes):
     vmem = pl.BlockSpec(memory_space=pltpu.VMEM)
     hbm = pl.BlockSpec(memory_space=pl.ANY)
     depth, width = weight.shape
@@ -574,12 +637,13 @@
             jax.ShapeDtypeStruct((1024, width), jnp.bfloat16),
             jax.ShapeDtypeStruct((1, 128), jnp.float32),
         ),
-        in_specs=[hbm, hbm, vmem, vmem, vmem, vmem],
+        in_specs=[hbm, hbm, vmem, pl.BlockSpec(memory_space=pltpu.SMEM), vmem],
         out_specs=(vmem, vmem),
         scratch_shapes=[
             pltpu.VMEM((4, 8, MERGED_DEV, depth // 4), jnp.bfloat16),
             pltpu.VMEM((depth, width), jnp.bfloat16),
             pltpu.VMEM((group, width), jnp.float32),
+            pltpu.VMEM((group, 128), jnp.int32),
             pltpu.VMEM((group, width), jnp.bfloat16),
             pltpu.VMEM((8, 128), jnp.float32),
             pltpu.VMEM((8, 8, 128), jnp.float32),
@@ -591,7 +655,7 @@
             collective_id=2, has_side_effects=True, vmem_limit_bytes=60 * 1024 * 1024
         ),
         name="merger",
-    )(merged, weight, gain, req, counts, routes)
+    )(merged, weight, gain, grid, routes)
 
 
 def per_device(
@@ -612,30 +676,20 @@
     n_rows = lax.axis_size("rows")
     n_mlp = lax.axis_size("mlp")
     member = lax.axis_index("mlp")
-    own_grid = lax.dynamic_slice_in_dim(grid_sides, member * REQ_DEV, REQ_DEV, 0)
-    token_index, is_valid, owner_slot, own_counts = merge_layout(own_grid)
-    token_index = jnp.where(is_valid[:, None], token_index, -1)
     merged = layer(
         tokens,
         norm_gain,
         norm_bias,
         input_weight,
-        input_bias[None, :],
+        input_bias,
         output_weight,
         expand_weight,
         reduce_weight,
-        segments[None, :],
-        token_index,
+        segments,
+        grid_sides,
     )
-    group_valid, group_owner, group_counts = jax.vmap(merge_layout)(
-        grid_sides.reshape(n_mlp, REQ_DEV, 2)
-    )[1:]
-    group_requests = n_mlp * REQ_DEV
-    member_base = (REQ_DEV * jnp.arange(n_mlp, dtype=jnp.int32))[:, None]
-    request_of_row = jnp.where(group_valid, group_owner + member_base, 128).reshape(-1, 1)
-    counts = jnp.pad(group_counts.reshape(1, -1).astype(jnp.float32), ((0, 0), (0, 128 - group_requests)))
     outgoing, peak_values = merger(
-        merged, merger_weight, output_gain[None, :], request_of_row, counts, routes
+        merged, merger_weight, output_gain, grid_sides, routes.reshape(1, -1)
     )
     peaks_own = lax.dynamic_slice_in_dim(peak_values[0], member * REQ_DEV, REQ_DEV, 0)
     capacity = outgoing.shape[0] // (n_rows * n_mlp)

time: 201 us -> 187 us (0.930)
  Pallas kernels: 167 us -> 159 us
  local copies, waits for them, and re-layouts: 9.15 us -> 4.23 us
    pallas_call x1, Pallas kernels: 124 us -> 116 us  [layer(): pl.pallas_call(layer_kernel, out_shape=jax.ShapeDtypeStruct((MERGED_DEV,...]
where the time goes in v3:
time: 187 us; the launch traced here: 186 us
  Pallas kernels  159 us (85%)
  waiting for transfers between devices  17.8 us (10%)
  starting transfers between devices  4.28 us (2%)
  local copies, waits for them, and re-layouts  4.23 us (2%)
    pallas_call x1, Pallas kernels, layer(): pl.pallas_call(layer_kernel, out_shape=jax.ShapeDtypeStruct((MERGED_DEV,...  116 us
    pallas_call x1, Pallas kernels, merger(): pl.pallas_call(merger_kernel, out_shape=(jax.ShapeDtypeStruct((1024, widt...  43.8 us
    all_to_all x1, waiting for transfers between devices, per_device(): lax.all_to_all(outgoing, ('rows', 'mlp'), split_axis=0, concat_axis=0, ti...  17.8 us
    all_to_all x1, starting transfers between devices, per_device(): lax.all_to_all(outgoing, ('rows', 'mlp'), split_axis=0, concat_axis=0, ti...  4.28 us
  transfers between devices with their start and end apart: 1, of which 1 were waited for; matrix products, arithmetic and copies ran while one was open for 1% of the time, Pallas kernels for 0%

profile of v3, /device:TPU:1, one launch (start us, length us, event | category | flops | bytes accessed | tf_op | source)
XLA Modules:
  0.0 186.3 jit_solution(9522780492069232523)
XLA Ops:
  0.6 1.4 copy.15.grid
  2.0 115.6 %layer.1.merged = bf16[64,5632]{1,0:T(8,128)(2,1)} custom-call(bf16[256,1408]{1,0:T(8,128)(2,1)} %tokens.1, f32[3,1408]{1,0:T(4,128)} %gain.2, f32[3,1408]{1,0:T(4,128)} %bias.1, bf16[1408,4224]{1,0:T(8,128)(2,1)} %wq_hbm.1, f32[4224]{0:T(1024)} %bq.1, bf16[1408,1408]{1,0:T(8,128)(2,1)} %wo_hbm.1, bf16[384,1408]{1,0:T(8,128)(2,1)} %wa_hbm.1, ...), custom_call_target="tpu_custom_call" | custom-call | tf_op jit(solution)/shard_map/layer/pallas_call | solution.py:422
  117.6 43.8 %merger.1 = (bf16[1024,512]{1,0:T(8,128)(2,1)}, f32[1,128]{1,0:T(1,128)}) custom-call(bf16[64,5632]{1,0:T(8,128)(2,1)} %layer.1.merged, bf16[5632,512]{1,0:T(8,128)(2,1)} %w_hbm.1, f32[512]{0:T(512)} %gain.3, s32[32,2]{1,0:T(8,128)} %copy.15.grid, s32[1,512]{1,0:T(1,128)} %bitcast.13), custom_call_target="tpu_custom_call" | custom-call | tf_op jit(solution)/shard_map/merger/pallas_call | solution.py:634
  161.3 4.3 %all-to-all-start = ((bf16[128,8,512]{2,1,0:T(8,128)(2,1)}), bf16[128,8,512]{2,1,0:T(8,128)(2,1)S(1)}, u32[]{:S(2)}, u32[]{:S(2)}) async-start(bf16[128,8,512]{2,1,0:T(8,128)(2,1)} %bitcast.11), calls=%async_computation | async-start | bytes 2097152 | tf_op jit(solution)/shard_map/all_to_all | solution.py:697
  165.6 1.2 dynamic-slice_bitcast_fusion
  166.8 17.8 %all-to-all-done = bf16[128,8,512]{2,1,0:T(8,128)(2,1)S(1)} async-done(((bf16[128,8,512]{2,1,0:T(8,128)(2,1)}), bf16[128,8,512]{2,1,0:T(8,128)(2,1)S(1)}, u32[]{:S(2)}, u32[]{:S(2)}) %all-to-all-start) | async-done | bytes 1048608 | tf_op jit(solution)/shard_map/all_to_all | solution.py:697
  184.6 0.3 copy.17
  185.0 1.4 copy.18
Async XLA Ops:
  161.3 23.3 %all-to-all-start = ((bf16[128,8,512]{2,1,0:T(8,128)(2,1)}), bf16[128,8,512]{2,1,0:T(8,128)(2,1)S(1)}, u32[]{:S(2)}, u32[]{:S(2)}) async-start(bf16[128,8,512]{2,1,0:T(8,128)(2,1)} %bitcast.11), calls=%async_computation | async-start | bytes 2097152 | tf_op jit(solution)/shard_map/all_to_all | solution.py:697

commit v4 on v3

--- a/solution.py
+++ b/solution.py
@@ -24,7 +24,7 @@
     spans = []
     token, merge = 0, 0
     for k in range(REQ_DEV):
-        height, width = grid[first + k, 0], grid[first + k, 1]
+        height, width = grid[0, first + k], grid[1, first + k]
         count = lax.div(height, 2) * lax.div(width, 2)
         spans.append((height, width, token, merge, count))
         token = token + jnp.where(height > 0, 1 + height * width, 0)
@@ -453,8 +453,9 @@
 
 
 def merger_kernel(
-    merged, w_hbm, gain, grid, routes, outgoing, peaks,
-    blocks, weight, acc, req, scaled, stats, gathered, send, recv, local,
+    merged, w_hbm, gain, grid, routes, inbox, peaks,
+    blocks, weight, acc, req, scaled, stats, gathered, outgoing, send, recv, local,
+    post, mail, entered,
 ):
     row = lax.axis_index("rows")
     member = lax.axis_index("mlp")
@@ -486,7 +487,15 @@
         pl.semaphore_signal(
             barrier, inc=1, device_id=(row, (member + step) % 8), device_id_type=MESH
         )
-    pl.semaphore_wait(barrier, 7)
+    for step in range(1, 16):
+        pl.semaphore_signal(
+            barrier, inc=1, device_id=((row + step) % 16, member), device_id_type=MESH
+        )
+    pl.semaphore_wait(barrier, 22)
+    for step in range(1, 16):
+        pl.semaphore_signal(
+            entered, inc=1, device_id=((row + step) % 16, member), device_id_type=MESH
+        )
 
     sent = []
 
@@ -601,7 +610,9 @@
         total = total + gathered[m, 0:1, :]
         top = jnp.maximum(top, gathered[m, 1:2, :])
     inv_rms = lax.rsqrt(total / (jnp.maximum(number, 1.0) * OUT) + EPS)
-    peaks[...] = jnp.where(number > 0.0, top * inv_rms, 0.0)
+    highest = jnp.where(number > 0.0, top * inv_rms, 0.0)
+    own_slots = pltpu.roll(jnp.broadcast_to(highest, (8, 128)), (128 - member * REQ_DEV) % 128, 1)
+    peaks[...] = own_slots[0, 0:REQ_DEV]
 
     def scale(t, carry):
         at = pl.ds(pl.multiple_of(t * MERGED_DEV, MERGED_DEV), MERGED_DEV)
@@ -611,16 +622,49 @@
 
     lax.fori_loop(0, 8, scale, 0)
 
-    def route(t, carry):
-        at = pl.multiple_of(t * 256, 256)
-        slot = lax.broadcasted_iota(jnp.int32, (256, group), 0) + at
+    me = row * 8 + member
+    here_x = row // 4
+
+    def route(t):
+        first = (here_x + t) % 4 * 32
+        slot = lax.broadcasted_iota(jnp.int32, (256, group), 0) + first * 8
         pick = (slot == key).astype(jnp.bfloat16)
-        outgoing[pl.ds(at, 256), :] = jnp.dot(
+        outgoing[pl.ds(first, 32)] = jnp.dot(
             pick, scaled[...], preferred_element_type=jnp.float32
-        ).astype(jnp.bfloat16)
-        return carry
-
-    lax.fori_loop(0, outgoing.shape[0] // 256, route, 0)
+        ).astype(jnp.bfloat16).reshape(32, 8, acc.shape[1])
+
+    def letter(t, n):
+        to = (here_x + t) % 4 * 32 + (me % 32 + n) % 32
+        return pltpu.make_async_remote_copy(
+            src_ref=outgoing.at[to], dst_ref=inbox.at[me],
+            send_sem=post.at[t * 32 + n], recv_sem=mail.at[t * 32 + n],
+            device_id=(to // 8, to % 8), device_id_type=MESH,
+        )
+
+    def mail_out(t):
+        def body(n, carry):
+            letter(t, n).start()
+            return carry
+
+        lax.fori_loop(1 if t == 0 else 0, 32, body, 0)
+
+    route(1)
+    pl.semaphore_wait(entered, 15)
+    for n, t in enumerate((1, 3, 2, 0)):
+        if n < 3:
+            route((3, 2, 0)[n])
+        mail_out(t)
+    keep = pltpu.make_async_copy(outgoing.at[me], inbox.at[me], local.at[0])
+    keep.start()
+    for t in (1, 3, 2, 0):
+        def settle(n, carry, t=t):
+            copy = letter(t, n)
+            copy.wait_send()
+            copy.wait_recv()
+            return carry
+
+        lax.fori_loop(1 if t == 0 else 0, 32, settle, 0)
+    keep.wait()
     for copy in sent:
         copy.wait_send()
 
@@ -634,11 +678,11 @@
     return pl.pallas_call(
         merger_kernel,
         out_shape=(
-            jax.ShapeDtypeStruct((1024, width), jnp.bfloat16),
-            jax.ShapeDtypeStruct((1, 128), jnp.float32),
+            jax.ShapeDtypeStruct((128, 8, width), jnp.bfloat16),
+            jax.ShapeDtypeStruct((REQ_DEV,), jnp.float32),
         ),
         in_specs=[hbm, hbm, vmem, pl.BlockSpec(memory_space=pltpu.SMEM), vmem],
-        out_specs=(vmem, vmem),
+        out_specs=(hbm, vmem),
         scratch_shapes=[
             pltpu.VMEM((4, 8, MERGED_DEV, depth // 4), jnp.bfloat16),
             pltpu.VMEM((depth, width), jnp.bfloat16),
@@ -647,9 +691,13 @@
             pltpu.VMEM((group, width), jnp.bfloat16),
             pltpu.VMEM((8, 128), jnp.float32),
             pltpu.VMEM((8, 8, 128), jnp.float32),
+            pltpu.VMEM((128, 8, width), jnp.bfloat16),
             pltpu.SemaphoreType.DMA((copies,)),
             pltpu.SemaphoreType.DMA((copies,)),
             pltpu.SemaphoreType.DMA((8,)),
+            pltpu.SemaphoreType.DMA((128,)),
+            pltpu.SemaphoreType.DMA((128,)),
+            pltpu.SemaphoreType.REGULAR,
         ],
         compiler_params=pltpu.CompilerParams(
             collective_id=2, has_side_effects=True, vmem_limit_bytes=60 * 1024 * 1024
@@ -675,7 +723,7 @@
 ):
     n_rows = lax.axis_size("rows")
     n_mlp = lax.axis_size("mlp")
-    member = lax.axis_index("mlp")
+    sides = grid_sides.T
     merged = layer(
         tokens,
         norm_gain,
@@ -686,17 +734,13 @@
         expand_weight,
         reduce_weight,
         segments,
-        grid_sides,
+        sides,
     )
-    outgoing, peak_values = merger(
-        merged, merger_weight, output_gain, grid_sides, routes.reshape(1, -1)
+    arrived, peaks_own = merger(
+        merged, merger_weight, output_gain, sides, routes.reshape(1, -1)
     )
-    peaks_own = lax.dynamic_slice_in_dim(peak_values[0], member * REQ_DEV, REQ_DEV, 0)
-    capacity = outgoing.shape[0] // (n_rows * n_mlp)
-    outgoing = outgoing.reshape(n_rows * n_mlp, capacity, -1)
-    arrived = lax.all_to_all(outgoing, ("rows", "mlp"), split_axis=0, concat_axis=0, tiled=True)
-    arrived = arrived.reshape(n_rows, n_mlp, capacity, -1)
-    delivered = arrived.transpose(2, 0, 1, 3).reshape(capacity * n_rows, -1)
+    arrived = arrived.reshape(n_rows, n_mlp, arrived.shape[1], -1)
+    delivered = arrived.transpose(2, 0, 1, 3).reshape(arrived.shape[2] * n_rows, -1)
     return (delivered, peaks_own)
 
 

time: 187 us -> 180 us (0.963)
  waiting for transfers between devices: 17.8 us -> 0 us
  Pallas kernels: 159 us -> 176 us
  starting transfers between devices: 4.28 us -> 0 us
    all_to_all x1 -> x0, waiting for transfers between devices: 17.8 us -> none  [per_device(): lax.all_to_all(outgoing, ('rows', 'mlp'), split_axis=0, concat_axis=0, ti...]
    pallas_call x1, Pallas kernels: 43.8 us -> 60.6 us  [merger(): pl.pallas_call(merger_kernel, out_shape=(jax.ShapeDtypeStruct((128, 8, wi...]
    all_to_all x1 -> x0, starting transfers between devices: 4.28 us -> none  [per_device(): lax.all_to_all(outgoing, ('rows', 'mlp'), split_axis=0, concat_axis=0, ti...]
  transfers between devices with their start and end apart: 1 -> 0, of which waited for: 1 -> 0; matrix products, arithmetic and copies ran while one was open for 1% -> 0% of each run, Pallas kernels for 0% -> 0%
where the time goes in v4:
time: 180 us
  Pallas kernels  176 us (98%)
  local copies, waits for them, and re-layouts  3.41 us (2%)
    pallas_call x1, Pallas kernels, layer(): pl.pallas_call(layer_kernel, out_shape=jax.ShapeDtypeStruct((MERGED_DEV,...  116 us
    pallas_call x1, Pallas kernels, merger(): pl.pallas_call(merger_kernel, out_shape=(jax.ShapeDtypeStruct((128, 8, wi...  60.6 us

profile of v4, /device:TPU:1, one launch (start us, length us, event | category | flops | bytes accessed | tf_op | source)
XLA Modules:
  0.0 180.3 jit_solution(2259841761828273418)
XLA Ops:
  0.6 115.6 %layer.1.merged = bf16[64,5632]{1,0:T(8,128)(2,1)} custom-call(bf16[256,1408]{1,0:T(8,128)(2,1)} %tokens.1, f32[3,1408]{1,0:T(4,128)} %gain.2, f32[3,1408]{1,0:T(4,128)} %bias.1, bf16[1408,4224]{1,0:T(8,128)(2,1)} %wq_hbm.1, f32[4224]{0:T(1024)} %bq.1, bf16[1408,1408]{1,0:T(8,128)(2,1)} %wo_hbm.1, bf16[384,1408]{1,0:T(8,128)(2,1)} %wa_hbm.1, ...), custom_call_target="tpu_custom_call" | custom-call | tf_op jit(solution)/shard_map/layer/pallas_call | solution.py:422
  116.3 60.6 %merger.1 = (bf16[128,8,512]{2,1,0:T(8,128)(2,1)}, f32[4]{0:T(128)}) custom-call(bf16[64,5632]{1,0:T(8,128)(2,1)} %layer.1.merged, bf16[5632,512]{1,0:T(8,128)(2,1)} %w_hbm.1, f32[512]{0:T(512)} %gain.3, s32[2,32]{1,0:T(2,128)} %bitcast.12, s32[1,512]{1,0:T(1,128)} %bitcast.13), custom_call_target="tpu_custom_call" | custom-call | tf_op jit(solution)/shard_map/merger/pallas_call | solution.py:678
  176.9 0.0 copy-start
  176.9 1.5 copy.15
  178.4 1.4 copy.16
  179.8 0.0 copy-done
  179.8 0.5 copy.18
Async XLA Ops:
  176.9 2.9 %copy-start = (f32[4]{0:T(128)S(1)}, f32[4]{0:T(128)}, u32[]{:S(2)}) copy-start(f32[4]{0:T(128)} %get-tuple-element.9) | copy-start | bytes 52

commit v5 on v4

--- a/solution.py
+++ b/solution.py
@@ -39,9 +39,9 @@
 
 
 def layer_kernel(
-    tokens, gain, bias, wq_hbm, bq, wo_hbm, wa_hbm, wb_hbm, seg, grid, merged_out,
+    tokens, gain, bias, wq_hbm, bq, wo_hbm, wa_hbm, wb_hbm, seg, grid, w_hbm,
     wa, wb, wq, wo, joint, acts, resid, acc, att, maskb, pick, psend, precv,
-    send, recv, local,
+    send, recv, local, blocks, entered,
 ):
     row = lax.axis_index("rows")
     member = lax.axis_index("mlp")
@@ -58,7 +58,8 @@
         return (row, ((y + dy + 4) % 4) * 2 + core)
 
     partner = (row, member + 1 - 2 * core)
-    near = [plane(1, 0), plane(-1, 0), plane(0, 1), plane(0, -1), column(1), column(-1), partner]
+    row_peers = [((row + step) % 16, member) for step in range(1, 16)]
+    near = [(row, (member + step) % 8) for step in range(1, 8)] + row_peers
 
     started = []
 
@@ -171,6 +172,8 @@
         table["s1", n] = send_first(w)
     for n, w in enumerate(weights):
         table["s2", n, 0] = send_second(w, 0)
+    for device in row_peers:
+        pl.semaphore_signal(entered, inc=1, device_id=device, device_id_type=MESH)
 
     passing = []
 
@@ -213,7 +216,7 @@
             arrived(table["f2", n, i])
         spread([(n, i, 2) for n in (0, 1)])
 
-    def norm_rows(read, write, i):
+    def norm_rows(read, write, i, begin=0, end=rows_here):
         def body(t, carry):
             at = pl.ds(pl.multiple_of(t * 32, 32), 32)
             value = read(at)
@@ -223,7 +226,7 @@
             write(at, centered * lax.rsqrt(variance + EPS) * gain[i : i + 1, :] + bias[i : i + 1, :])
             return carry
 
-        lax.fori_loop(0, rows_here // 32, body, 0, unroll=2)
+        lax.fori_loop(begin // 32, end // 32, body, 0, unroll=2)
 
     def write_acts(at, value):
         acts[at, :] = value.astype(jnp.bfloat16)
@@ -265,6 +268,11 @@
 
     lax.fori_loop(0, parts, project, 0)
     service_first()
+    width = w_hbm.shape[1]
+    fetched = [
+        load(w_hbm.at[pl.ds(q * features, features)], wq.at[:, pl.ds(q * width, width)])
+        for q in range(4)
+    ]
     pick_rows()
 
     contract = (((1,), (1,)), ((), ()))
@@ -371,21 +379,24 @@
         10: before_10, 11: before_11, 12: before_12, 13: before_13, 14: before_14, 15: before_15,
     }
 
+    def ffn_rows(i, k, begin, end):
+        pre = lax.dot_general(acts[begin:end, :], wa[k, i], contract, preferred_element_type=jnp.float32)
+        hidden = (0.5 * pre * (1.0 + lax.erf(pre * math.sqrt(0.5)))).astype(jnp.bfloat16)
+        for start, width in ((0, 512), (512, 512), (1024, 384)):
+            acc[begin:end, start : start + width] += jnp.dot(
+                hidden, wb[k, i, :, start : start + width], preferred_element_type=jnp.float32
+            )
+
     def ffn(t, carry):
         code = zero
         for n, (i, k) in enumerate(order):
             code = jnp.where(t == n, i * 4 + k, code)
         i, k = code // 4, code % 4
-        pre = lax.dot_general(acts[...], wa[k, i], contract, preferred_element_type=jnp.float32)
-        hidden = (0.5 * pre * (1.0 + lax.erf(pre * math.sqrt(0.5)))).astype(jnp.bfloat16)
-        for start, width in ((0, 512), (512, 512), (1024, 384)):
-            acc[:, start : start + width] += jnp.dot(
-                hidden, wb[k, i, :, start : start + width], preferred_element_type=jnp.float32
-            )
+        ffn_rows(i, k, 0, 2 * rows_here)
         return carry
 
     begun = 0
-    for n in [*sorted(services), len(order)]:
+    for n in sorted(services):
         lax.fori_loop(begun, n, ffn, 0)
         if n in services:
             services[n]()
@@ -396,64 +407,42 @@
         psend[pl.ds(at, 32), :] = acc[pl.ds(rows_here + at, 32), :].astype(jnp.bfloat16)
         return carry
 
-    lax.fori_loop(0, rows_here // 32, narrow, 0)
-    back = push(psend, precv, partner)
-    back.wait_recv()
+    last_i, last_k = order[-1]
+    ffn_rows(last_i, last_k, rows_here, 2 * rows_here)
+    piece = rows_here // 4
+    back = []
+
+    def hand_over(p):
+        at = pl.ds(p * piece, piece)
+        back.append(push(psend.at[at], precv.at[at], partner))
+
+    for p in range(4):
+        lax.fori_loop(p * piece // 32, (p + 1) * piece // 32, narrow, 0)
+        if p >= 1:
+            hand_over(p - 1)
+    hand_over(3)
+    ffn_rows(last_i, last_k, 0, rows_here)
 
     def write_att(at, value):
         att[at, 0:features] = value.astype(jnp.bfloat16)
 
-    norm_rows(
-        lambda at: resid[at, :] + (acc[at, :] + precv[at, :].astype(jnp.float32)), write_att, 2
-    )
-    for q in range(4):
-        merged_out[:, q * features : (q + 1) * features] = jnp.dot(
+    for p in range(4):
+        back[p].wait_recv()
+        norm_rows(
+            lambda at: resid[at, :] + (acc[at, :] + precv[at, :].astype(jnp.float32)),
+            write_att, 2, p * piece, (p + 1) * piece,
+        )
+
+    def produce(q):
+        blocks[q, member] = jnp.dot(
             pick[q], att[:, 0:features], preferred_element_type=jnp.float32
         ).astype(jnp.bfloat16)
-    for copy in sent:
-        copy.wait_send()
-
-
-def layer(tokens, gain, bias, wq, bq, wo, wa, wb, seg, grid):
-    rows_here, features = tokens.shape
-    vmem = pl.BlockSpec(memory_space=pltpu.VMEM)
-    hbm = pl.BlockSpec(memory_space=pl.ANY)
-    copies = 2 * (2 + 2 + 16) + 90 + 2
-    return pl.pallas_call(
-        layer_kernel,
-        out_shape=jax.ShapeDtypeStruct((MERGED_DEV, 4 * features), jnp.bfloat16),
-        in_specs=[
-            vmem, vmem, vmem, hbm, vmem, hbm, hbm, hbm, vmem,
-            pl.BlockSpec(memory_space=pltpu.SMEM),
-        ],
-        out_specs=vmem,
-        scratch_shapes=[
-            pltpu.VMEM((4, 4, SLOT, features), jnp.bfloat16),
-            pltpu.VMEM((4, 4, SLOT, features), jnp.bfloat16),
-            pltpu.VMEM((features, 3 * features), jnp.bfloat16),
-            pltpu.VMEM((features, features), jnp.bfloat16),
-            pltpu.VMEM((rows_here, 3 * features + 128), jnp.bfloat16),
-            pltpu.VMEM((2 * rows_here, features), jnp.bfloat16),
-            pltpu.VMEM((rows_here, features), jnp.float32),
-            pltpu.VMEM((2 * rows_here, features), jnp.float32),
-            pltpu.VMEM((rows_here, features + 128), jnp.bfloat16),
-            pltpu.VMEM((rows_here, rows_here), jnp.float32),
-            pltpu.VMEM((4, MERGED_DEV, rows_here), jnp.bfloat16),
-            pltpu.VMEM((rows_here, features), jnp.bfloat16),
-            pltpu.VMEM((rows_here, features), jnp.bfloat16),
-            pltpu.SemaphoreType.DMA((copies,)),
-            pltpu.SemaphoreType.DMA((copies,)),
-            pltpu.SemaphoreType.DMA((22,)),
-        ],
-        compiler_params=pltpu.CompilerParams(
-            collective_id=1, has_side_effects=True, vmem_limit_bytes=60 * 1024 * 1024
-        ),
-        name="layer",
-    )(tokens, gain, bias, wq, bq, wo, wa, wb, seg, grid)
+
+    return produce, fetched, sent
 
 
 def merger_kernel(
-    merged, w_hbm, gain, grid, routes, inbox, peaks,
+    produce, fetched, gain, grid, routes, inbox, peaks,
     blocks, weight, acc, req, scaled, stats, gathered, outgoing, send, recv, local,
     post, mail, entered,
 ):
@@ -461,41 +450,12 @@
     member = lax.axis_index("mlp")
     y, core = member // 2, member % 2
     parts = 4
-    depth = w_hbm.shape[0] // parts
+    depth, width = blocks.shape[3], acc.shape[1]
     group = 8 * MERGED_DEV
 
     def at_y(dy, other=False):
         side = 1 - core if other else core
         return ((y + dy + 4) % 4) * 2 + side
-
-    started = []
-    for q in range(parts):
-        copy = pltpu.make_async_copy(
-            merged.at[:, pl.ds(q * depth, depth)], blocks.at[q, member], local.at[q]
-        )
-        copy.start()
-        started.append(copy)
-    fetched = []
-    for q in range(parts):
-        rows_q = pl.ds(q * depth, depth)
-        copy = pltpu.make_async_copy(w_hbm.at[rows_q], weight.at[rows_q], local.at[parts + q])
-        copy.start()
-        fetched.append(copy)
-
-    barrier = pltpu.get_barrier_semaphore()
-    for step in range(1, 8):
-        pl.semaphore_signal(
-            barrier, inc=1, device_id=(row, (member + step) % 8), device_id_type=MESH
-        )
-    for step in range(1, 16):
-        pl.semaphore_signal(
-            barrier, inc=1, device_id=((row + step) % 16, member), device_id_type=MESH
-        )
-    pl.semaphore_wait(barrier, 22)
-    for step in range(1, 16):
-        pl.semaphore_signal(
-            entered, inc=1, device_id=((row + step) % 16, member), device_id_type=MESH
-        )
 
     sent = []
 
@@ -511,14 +471,13 @@
 
     half = MERGED_DEV // 2
     up, low = pl.ds(0, half), pl.ds(half, half)
-    first = []
+    first, swap = [], []
+    produce(0)
     for q in range(parts):
-        started[q].wait()
+        if q + 1 < parts:
+            produce(q + 1)
         mine = blocks.at[q, member]
         first.append([push(mine, mine, at_y(1)), push(mine, mine, at_y(-1))])
-    swap = []
-    for q in range(parts):
-        mine = blocks.at[q, member]
         swap.append([push(mine, mine, at_y(0, True))])
 
     target_row = routes[...]
@@ -569,7 +528,7 @@
                 cols = pl.ds(pl.multiple_of(n * 256, 256), 256)
                 value = jnp.dot(
                     blocks[p].reshape(group, depth),
-                    weight[p * depth : (p + 1) * depth, cols],
+                    weight[:, pl.ds(pl.multiple_of(p * width + n * 256, 256), 256)],
                     preferred_element_type=jnp.float32,
                 )
                 if p == 0:
@@ -669,41 +628,77 @@
         copy.wait_send()
 
 
-def merger(merged, weight, gain, grid, routes):
+def whole_kernel(
+    tokens, gain, bias, wq_hbm, bq, wo_hbm, wa_hbm, wb_hbm, seg, grid, w_hbm, out_gain, routes,
+    inbox, peaks, *scratch,
+):
+    wq, blocks, entered = scratch[2], scratch[16], scratch[17]
+    produce, fetched, sent = layer_kernel(
+        tokens, gain, bias, wq_hbm, bq, wo_hbm, wa_hbm, wb_hbm, seg, grid, w_hbm, *scratch[:18]
+    )
+    merger_kernel(
+        produce, fetched, out_gain, grid, routes, inbox, peaks,
+        blocks, wq, *scratch[18:], entered,
+    )
+    for copy in sent:
+        copy.wait_send()
+
+
+def whole(tokens, gain, bias, wq, bq, wo, wa, wb, seg, grid, weight, out_gain, routes):
+    rows_here, features = tokens.shape
     vmem = pl.BlockSpec(memory_space=pltpu.VMEM)
     hbm = pl.BlockSpec(memory_space=pl.ANY)
-    depth, width = weight.shape
+    smem = pl.BlockSpec(memory_space=pltpu.SMEM)
+    width = weight.shape[1]
     group = 8 * MERGED_DEV
-    copies = 32 + 7
+    copies = 2 * (2 + 2 + 16) + 90 + 5
+    merger_copies = 32 + 7
     return pl.pallas_call(
-        merger_kernel,
+        whole_kernel,
         out_shape=(
             jax.ShapeDtypeStruct((128, 8, width), jnp.bfloat16),
             jax.ShapeDtypeStruct((REQ_DEV,), jnp.float32),
         ),
-        in_specs=[hbm, hbm, vmem, pl.BlockSpec(memory_space=pltpu.SMEM), vmem],
+        in_specs=[
+            vmem, vmem, vmem, hbm, vmem, hbm, hbm, hbm, vmem, smem, hbm, vmem, vmem,
+        ],
         out_specs=(hbm, vmem),
         scratch_shapes=[
-            pltpu.VMEM((4, 8, MERGED_DEV, depth // 4), jnp.bfloat16),
-            pltpu.VMEM((depth, width), jnp.bfloat16),
+            pltpu.VMEM((4, 4, SLOT, features), jnp.bfloat16),
+            pltpu.VMEM((4, 4, SLOT, features), jnp.bfloat16),
+            pltpu.VMEM((features, 3 * features), jnp.bfloat16),
+            pltpu.VMEM((features, features), jnp.bfloat16),
+            pltpu.VMEM((rows_here, 3 * features + 128), jnp.bfloat16),
+            pltpu.VMEM((2 * rows_here, features), jnp.bfloat16),
+            pltpu.VMEM((rows_here, features), jnp.float32),
+            pltpu.VMEM((2 * rows_here, features), jnp.float32),
+            pltpu.VMEM((rows_here, features + 128), jnp.bfloat16),
+            pltpu.VMEM((rows_here, rows_here), jnp.float32),
+            pltpu.VMEM((4, MERGED_DEV, rows_here), jnp.bfloat16),
+            pltpu.VMEM((rows_here, features), jnp.bfloat16),
+            pltpu.VMEM((rows_here, features), jnp.bfloat16),
+            pltpu.SemaphoreType.DMA((copies,)),
+            pltpu.SemaphoreType.DMA((copies,)),
+            pltpu.SemaphoreType.DMA((26,)),
+            pltpu.VMEM((4, 8, MERGED_DEV, features), jnp.bfloat16),
+            pltpu.SemaphoreType.REGULAR,
             pltpu.VMEM((group, width), jnp.float32),
             pltpu.VMEM((group, 128), jnp.int32),
             pltpu.VMEM((group, width), jnp.bfloat16),
             pltpu.VMEM((8, 128), jnp.float32),
             pltpu.VMEM((8, 8, 128), jnp.float32),
             pltpu.VMEM((128, 8, width), jnp.bfloat16),
-            pltpu.SemaphoreType.DMA((copies,)),
-            pltpu.SemaphoreType.DMA((copies,)),
+            pltpu.SemaphoreType.DMA((merger_copies,)),
+            pltpu.SemaphoreType.DMA((merger_copies,)),
             pltpu.SemaphoreType.DMA((8,)),
             pltpu.SemaphoreType.DMA((128,)),
             pltpu.SemaphoreType.DMA((128,)),
-            pltpu.SemaphoreType.REGULAR,
         ],
         compiler_params=pltpu.CompilerParams(
-            collective_id=2, has_side_effects=True, vmem_limit_bytes=60 * 1024 * 1024
+            collective_id=1, has_side_effects=True, vmem_limit_bytes=60 * 1024 * 1024
         ),
-        name="merger",
-    )(merged, weight, gain, grid, routes)
+        name="whole",
+    )(tokens, gain, bias, wq, bq, wo, wa, wb, seg, grid, weight, out_gain, routes)
 
 
 def per_device(
@@ -724,7 +719,7 @@
     n_rows = lax.axis_size("rows")
     n_mlp = lax.axis_size("mlp")
     sides = grid_sides.T
-    merged = layer(
+    arrived, peaks_own = whole(
         tokens,
         norm_gain,
         norm_bias,
@@ -735,9 +730,9 @@
         reduce_weight,
         segments,
         sides,
-    )
-    arrived, peaks_own = merger(
-        merged, merger_weight, output_gain, sides, routes.reshape(1, -1)
+        merger_weight,
+        output_gain,
+        routes.reshape(1, -1),
     )
     arrived = arrived.reshape(n_rows, n_mlp, arrived.shape[1], -1)
     delivered = arrived.transpose(2, 0, 1, 3).reshape(arrived.shape[2] * n_rows, -1)

time: 180 us -> 176 us (0.978)
  Pallas kernels: 176 us -> 171 us
    pallas_call x2 -> x1, Pallas kernels: 176 us -> 171 us  [whole(): pl.pallas_call(whole_kernel, out_shape=(jax.ShapeDtypeStruct((128, 8, wid...]
where the time goes in v5:
time: 176 us
  Pallas kernels  171 us (97%)
  local copies, waits for them, and re-layouts  3.41 us (2%)
    pallas_call x1, Pallas kernels, whole(): pl.pallas_call(whole_kernel, out_shape=(jax.ShapeDtypeStruct((128, 8, wid...  171 us

profile of v5, /device:TPU:1, one launch (start us, length us, event | category | flops | bytes accessed | tf_op | source)
XLA Modules:
  0.0 175.5 jit_solution(7850969170668231659)
XLA Ops:
  0.6 171.4 %whole.1 = (bf16[128,8,512]{2,1,0:T(8,128)(2,1)}, f32[4]{0:T(128)}) custom-call(bf16[256,1408]{1,0:T(8,128)(2,1)} %tokens.1, f32[3,1408]{1,0:T(4,128)} %gain.1, f32[3,1408]{1,0:T(4,128)} %bias.1, bf16[1408,4224]{1,0:T(8,128)(2,1)} %wq_hbm.1, f32[4224]{0:T(1024)} %bq.1, bf16[1408,1408]{1,0:T(8,128)(2,1)} %wo_hbm.1, bf16[384,1408]{1,0:T(8,128)(2,1)} %wa_hbm.1, ...), custom_call_target="tpu_custom_call" | custom-call | tf_op jit(solution)/shard_map/whole/pallas_call | solution.py:656
  172.1 0.0 copy-start
  172.1 1.5 copy.15
  173.6 1.4 copy.16
  175.0 0.0 copy-done
  175.0 0.5 copy.18
Async XLA Ops:
  172.1 2.9 %copy-start = (f32[4]{0:T(128)S(1)}, f32[4]{0:T(128)}, u32[]{:S(2)}) copy-start(f32[4]{0:T(128)} %get-tuple-element.9) | copy-start | bytes 52
